TPU v7x, 128 devices: a whole 4x4x4 slice. The times are simulated.
128 devices in a mesh: wave: 16 (over y, x), atm: 8 (over z, core).
Axes of the slice: x: 4, y: 4, z: 4, core: 2. Of those that a mesh axis runs over, the one named last changes fastest.
Arguments:
- spectra: bfloat16 [1296, 262144], P(None, ('wave', 'atm')), may hold values from 0.049804688 to 2
- interact: bfloat16 [1296, 1296], replicated, may hold values from -0.15625 to 0.15625
- sea_mask: int32 [262144], P(('wave', 'atm')), may hold values 0 or 1
- sea_tile: int32 [262144], P(('wave', 'atm')), may hold values from 0 to 127, as said below
- push_list: int32 [128, 128, 32], P(('wave', 'atm')), may hold values from -1 to 8191, as said below
- neighbors: int32 [4, 262144], P(None, ('wave', 'atm')), may hold values from 0 to 3071, as said below
- air_wind: float32 [2, 512, 2048], P(None, 'atm', 'wave'), may hold values from -6 to 6
- diffusion: float32 [512, 2048], P('atm', 'wave'), may hold values from 0.04 to 0.2
Outputs:
- wave_spectra: bfloat16 [1296, 262144], P(None, ('wave', 'atm'))
- surface_wind: float32 [2, 512, 2048], P(None, 'atm', 'wave')
- roughness: float32 [512, 2048], P('atm', 'wave')
Inputs may be any that keep to these rules, and one draw needn't show every extreme that they name: `sea_tile`: tile t covers atmosphere rows from (t mod 8) * 64 and columns from (t div 8) * 128. In every block no tile lies above more than 32 of its points, and in every block some tile lies above exactly 32. `push_list`: entry [t, b, r] is the cell, row-major within tile t, under the r-th sea point of block b (in point order) whose tile is t, and -1 for r at or past the number of such points. `neighbors`: entries index the block's points extended by 512 points of each adjacent block: index 512 + i is the block's point i. West and east of point i are 512 + i - 1 and 512 + i + 1; south lies from i to 512 + i, north from 512 + i to 1024 + i.
All inputs are finite; a program needn't handle non-finite values. No bound on the sum of `sea_mask` on one device may be relied on, other than what follows from the above.
Results may differ from a plain program's by a relative error of at most 0.0046.
Values may be sent and summed in bfloat16 or wider, within the bound.
No kernel may reach another device: no remote copies, remote signals or barrier semaphores. Data moves between devices by JAX's collectives and lax.ppermute only.
A program may use at most 256 MiB of HBM per device.

v0:
```python
import math

import jax
import jax.numpy as jnp
import numpy as np
from jax import lax
from jax.experimental import pallas as pl
from jax.experimental.pallas import tpu as pltpu
from jax.sharding import PartitionSpec as P

ND = 36
NF = 36
K = ND * NF
H = 512
ATM_STEPS = 4
TW = 256
CH = 144
NCH = K // CH
HALF = 72
HALO_ROWS = K + 16
F32 = jnp.float32
BF16 = jnp.bfloat16
I32 = jnp.int32

S_TILES = (0, 1, 2, 4, 5, 6)
N_TILES = (2, 3, 4, 6, 7, 8)
PICK = 8 * len(S_TILES)


def row_tables():
    r = np.arange(HALF)
    d = r % ND
    angle = (d + 0.5) * (2.0 * math.pi / ND)
    up = np.power(1.1, r // ND)
    cosine, sine = np.cos(angle), np.sin(angle)
    reach = 0.7 / up
    rows = [
        up * cosine,
        up * sine,
        np.abs(reach * cosine),
        np.abs(reach * sine),
        np.abs(reach * cosine) + np.abs(reach * sine),
        (cosine > 0).astype(np.float64),
        (sine > 0).astype(np.float64),
    ]
    table = np.stack(rows).astype(np.float32)
    return np.ascontiguousarray(np.broadcast_to(table[:, :, None], table.shape + (128,)))


COS_POS = [bool(math.cos((d + 0.5) * 2.0 * math.pi / ND) > 0) for d in range(ND)]


def west_kind(tile):
    signs = {COS_POS[(8 * tile + s) % ND] for s in range(8)}
    return "both" if len(signs) == 2 else ("west" if True in signs else "east")


def iota(shape, dim):
    return lax.broadcasted_iota(I32, shape, dim)


def hot(mask):
    return jnp.where(mask, 1.0, 0.0).astype(BF16)


def contract(a, b, da, db):
    return lax.dot_general(a, b, (((da,), (db,)), ((), ())), preferred_element_type=F32)


def params(megabytes):
    return pltpu.CompilerParams(vmem_limit_bytes=megabytes << 20)


def cost(flops, data):
    return pl.CostEstimate(flops=flops, bytes_accessed=data, transcendentals=0)


def prepare_kernel(tile_ref, mask_ref, push_ref, first_ref, last_ref, pts_ref, pusht_ref, to_prev, to_next):
    blocks = push_ref.shape[0]
    points = tile_ref.shape[1]
    pusht_ref[...] = push_ref[...].astype(F32).T.astype(I32)
    before = hot(iota((TW, TW), 0) < iota((TW, TW), 1))
    ones = jnp.ones((TW, TW), BF16)
    running = jnp.zeros((blocks, TW), F32)
    for c in range(points // TW):
        cols = slice(c * TW, (c + 1) * TW)
        tile = tile_ref[:, cols]
        same = iota((blocks, TW), 0) == tile
        onehot = hot(same)
        earlier = contract(onehot, before, 1, 0) + running
        rank = jnp.sum(jnp.where(same, earlier, 0.0), axis=0, keepdims=True)
        running = running + contract(onehot, ones, 1, 0)
        pts_ref[0:1, cols] = tile.astype(F32)
        pts_ref[1:2, cols] = rank
        pts_ref[2:3, cols] = mask_ref[:, cols].astype(F32)
        pts_ref[3:8, cols] = jnp.zeros((5, TW), F32)
    for out, src, lo in ((to_prev, first_ref, 0), (to_next, last_ref, points - H)):
        out[:K, :] = src[...]
        rows = jnp.concatenate([pts_ref[:, lo : lo + H], jnp.zeros((8, H), F32)], axis=0)
        out[K:, :] = rows.astype(BF16)


def prepare(tile, mask, push, spectra):
    blocks, capacity = push.shape
    points = tile.shape[1]
    last = points // H - 1
    whole = lambda *shape: pl.BlockSpec(shape, lambda i: (0,) * len(shape))
    return pl.pallas_call(
        prepare_kernel,
        grid=(1,),
        in_specs=[
            whole(1, points),
            whole(1, points),
            whole(blocks, capacity),
            pl.BlockSpec((K, H), lambda i: (0, 0)),
            pl.BlockSpec((K, H), lambda i: (0, last)),
        ],
        out_specs=[whole(8, points), whole(capacity, blocks), whole(HALO_ROWS, H), whole(HALO_ROWS, H)],
        out_shape=[
            jax.ShapeDtypeStruct((8, points), F32),
            jax.ShapeDtypeStruct((capacity, blocks), I32),
            jax.ShapeDtypeStruct((HALO_ROWS, H), BF16),
            jax.ShapeDtypeStruct((HALO_ROWS, H), BF16),
        ],
        compiler_params=params(32),
        cost_estimate=cost(2 * 2 * blocks * TW * points, 4 * HALO_ROWS * H * 2),
        name="prepare",
    )(tile, mask, push, spectra, spectra)


def base_tile(interact, s_ref, mask, out_ref):
    out_ref[...] = jnp.dot(interact[...], s_ref[...], preferred_element_type=F32)
    for lane in range(TW // 128):
        lanes = slice(lane * 128, (lane + 1) * 128)
        acc = jnp.zeros((HALF, 128), F32)
        for m in range(NCH):
            s = s_ref[m * CH : (m + 1) * CH, lanes].astype(F32)
            acc = acc + (s[:HALF] + s[HALF:])
        mean = jnp.sum(acc, axis=0, keepdims=True) * (1.0 / K)
        msk = jnp.broadcast_to(mask[:, lanes], (8, 128))
        quota = jnp.broadcast_to(mean / (1.0 + mean), (8, 128)) * msk * 0.15
        half = 0.5 * msk
        low = iota((8, 128), 0) < 4
        for m in range(NCH):
            s = s_ref[m * CH : (m + 1) * CH, lanes].astype(F32)
            n = out_ref[m * CH : (m + 1) * CH, lanes]
            keeps = []
            for h in range(2):
                power = 1.21 ** (4 * m + 2 * h - NF / 2)
                a = msk - power * quota
                b = msk - (1.21 * power) * quota
                keeps += [a] * 4 + [jnp.where(low, a, b)] + [b] * 4
            out = [
                s[8 * i : 8 * i + 8] * keep + n[8 * i : 8 * i + 8] * half for i, keep in enumerate(keeps)
            ]
            out_ref[m * CH : (m + 1) * CH, lanes] = jnp.concatenate(out, axis=0)


def base_kernel(it_ref, s_ref, p_ref, out_ref):
    base_tile(it_ref, s_ref, p_ref[2:3, :], out_ref)


def base_own(interact, spectra, pts):
    points = spectra.shape[1]
    return pl.pallas_call(
        base_kernel,
        grid=(points // TW,),
        in_specs=[
            pl.BlockSpec((K, K), lambda i: (0, 0), pipeline_mode=pl.Buffered(1)),
            pl.BlockSpec((K, TW), lambda i: (0, i)),
            pl.BlockSpec((8, TW), lambda i: (0, i)),
        ],
        out_specs=pl.BlockSpec((K, TW), lambda i: (0, i)),
        out_shape=jax.ShapeDtypeStruct((K, points), F32),
        compiler_params=params(32),
        cost_estimate=cost(2 * K * K * points, K * K * 2 + K * points * 6),
        name="base_own",
    )(interact, spectra, pts)


def base_halo_kernel(it_ref, sb_ref, sa_ref, pb_ref, pa_ref, out_ref):
    i = pl.program_id(0)

    @pl.when(i < H // TW)
    def _():
        base_tile(it_ref, sb_ref, pb_ref[...].astype(F32)[2:3, :], out_ref)

    @pl.when(i >= H // TW)
    def _():
        base_tile(it_ref, sa_ref, pa_ref[...].astype(F32)[2:3, :], out_ref)


def base_halo(interact, before, after):
    n = H // TW
    early = lambda i: jnp.minimum(i, n - 1)
    late = lambda i: jnp.maximum(i - n, 0)
    return pl.pallas_call(
        base_halo_kernel,
        grid=(2 * n,),
        in_specs=[
            pl.BlockSpec((K, K), lambda i: (0, 0), pipeline_mode=pl.Buffered(1)),
            pl.BlockSpec((K, TW), lambda i: (0, early(i))),
            pl.BlockSpec((K, TW), lambda i: (0, late(i))),
            pl.BlockSpec((16, TW), lambda i: (K // 16, early(i))),
            pl.BlockSpec((16, TW), lambda i: (K // 16, late(i))),
        ],
        out_specs=pl.BlockSpec((K, TW), lambda i: (0, i)),
        out_shape=jax.ShapeDtypeStruct((K, 2 * H), F32),
        compiler_params=params(32),
        cost_estimate=cost(2 * K * K * 2 * H, K * K * 2 + K * 2 * H * 6),
        name="base_halo",
    )(interact, before, after, before, after)


def air_kernel(lat_total, mid_ref, left_ref, right_ref, pusht_ref, air_ref, out_ref, slots):
    rows = mid_ref.shape[1]
    lat_dev = rows - 16
    lane = iota((rows, 128), 1)

    def field(i):
        side = jnp.where(lane < 8, right_ref[i], jnp.where(lane >= 120, left_ref[i], 0.0))
        return jnp.concatenate([mid_ref[i], side], axis=1)

    east, north, spread = field(0), field(1), field(2)
    first = lax.axis_index("atm") * lat_dev - 8
    row = (iota((rows, 256), 0) + first).astype(F32)
    turning = 0.05 + 0.1 * row / lat_total

    def laplace(w):
        around = pltpu.roll(w, rows - 1, 0) + pltpu.roll(w, 1, 0) + pltpu.roll(w, 255, 1) + pltpu.roll(w, 1, 1)
        return around - 4.0 * w

    for _ in range(ATM_STEPS):
        e = east + spread * laplace(east) + turning * north
        n = north + spread * laplace(north) - turning * east
        east, north = e, n
    east = east[8 : 8 + lat_dev, :128]
    north = north[8 : 8 + lat_dev, :128]
    air_ref[0] = east
    air_ref[1] = north
    field_t = jnp.concatenate([east.T, north.T], axis=0).astype(BF16)
    capacity, blocks = pusht_ref.shape
    group = 4
    for g in range(capacity // group):
        cells = jnp.concatenate([pusht_ref[g * group + k : g * group + k + 1, :] for k in range(group)], axis=1)
        at_row = hot(iota((lat_dev, group * blocks), 0) == (cells >> 7))
        picked = jnp.dot(field_t, at_row, preferred_element_type=F32)
        at_col = iota((128, group * blocks), 0) == (cells & 127)
        for c in range(2):
            value = jnp.sum(jnp.where(at_col, picked[c * 128 : (c + 1) * 128], 0.0), axis=0, keepdims=True)
            for k in range(group):
                at = c * capacity + g * group + k
                slots[at : at + 1, :] = value[:, k * blocks : (k + 1) * blocks]
    own = slots[...]
    stacked = jnp.concatenate([pltpu.roll(own, 1, 1), own, pltpu.roll(own, blocks - 1, 1), jnp.zeros_like(own)], axis=0)
    out_ref[...] = stacked.T.reshape(out_ref.shape)


def air(lat_total, mid, left, right, pusht):
    capacity, blocks = pusht.shape
    lat_dev = mid.shape[1] - 16
    assert mid.shape[2] == 128 and blocks == 128
    return pl.pallas_call(
        lambda *refs: air_kernel(lat_total, *refs),
        out_shape=[
            jax.ShapeDtypeStruct((2, lat_dev, 128), F32),
            jax.ShapeDtypeStruct((blocks, 1, 8 * capacity), F32),
        ],
        scratch_shapes=[pltpu.VMEM((2 * capacity, blocks), F32)],
        compiler_params=params(24),
        cost_estimate=cost(2 * 256 * lat_dev * capacity * blocks, 600000),
        name="air",
    )(mid, left, right, pusht)


def winds_at(table, tile, rank):
    slots = table.shape[0] // 2
    tiles = table.shape[1]
    points = tile.shape[1]
    onehot = hot(iota((tiles, points), 0) == tile.astype(I32))
    values = jnp.dot(table, onehot, preferred_element_type=F32)
    at = iota((slots, points), 0) == rank.astype(I32)
    east = jnp.sum(jnp.where(at, values[:slots], 0.0), axis=0, keepdims=True)
    north = jnp.sum(jnp.where(at, values[slots:], 0.0), axis=0, keepdims=True)
    return east, north, onehot, at


def growth_pattern(tab_ref, east, north):
    return tab_ref[0] * (0.2 * east) + tab_ref[1] * (0.2 * north)


def step_scale(m, h):
    return 1.1 ** (4 * m + 2 * h - NF / 2)


def source_kernel(tab_ref, got_ref, s_ref, base_ref, p_ref, out_ref, send_ref, table, total):
    i = pl.program_id(0)

    @pl.when(i == 0)
    def _():
        got = got_ref[...].reshape(got_ref.shape[0], got_ref.shape[2])
        table[...] = got.T[64:128, :].astype(BF16)
        total[...] = jnp.zeros_like(total)

    mask = p_ref[2:3, :]
    east, north, onehot, at = winds_at(table[...], p_ref[0:1, :], p_ref[1:2, :])
    wave_x, wave_y = [], []
    for lane in range(TW // 128):
        lanes = slice(lane * 128, (lane + 1) * 128)
        pattern = growth_pattern(tab_ref, east[:, lanes] * mask[:, lanes], north[:, lanes] * mask[:, lanes])
        acc = jnp.zeros((HALF, 128), F32)
        for m in range(NCH):
            s = s_ref[m * CH : (m + 1) * CH, lanes].astype(F32)
            b = base_ref[m * CH : (m + 1) * CH, lanes]
            out = []
            for h in range(2):
                scale = step_scale(m, h)
                half = slice(h * HALF, (h + 1) * HALF)
                grown = jnp.maximum(pattern - 0.25 / scale, 0.0) * s[half]
                out.append(b[half] + scale * grown)
                acc = acc + (scale * scale) * grown
            out_ref[m * CH : (m + 1) * CH, lanes] = jnp.concatenate(out, axis=0).astype(BF16)
        wave_x.append(jnp.sum(acc * tab_ref[0], axis=0, keepdims=True))
        wave_y.append(jnp.sum(acc * tab_ref[1], axis=0, keepdims=True))
    wave_x = jnp.concatenate(wave_x, axis=1) * (0.4 / K)
    wave_y = jnp.concatenate(wave_y, axis=1) * (0.4 / K)
    speed = jnp.sqrt(east * east + north * north + 0.25)
    stress_x = mask * (0.3 * speed * east + wave_x)
    stress_y = mask * (0.3 * speed * north + wave_y)
    rough = mask * 0.2 * jnp.sqrt(stress_x * stress_x + stress_y * stress_y + 0.01)
    values = jnp.concatenate([jnp.where(at, v, 0.0) for v in (stress_x, stress_y, rough, mask)], axis=0)
    high = values.astype(BF16)
    rest = values - high.astype(F32)
    middle = rest.astype(BF16)
    low = (rest - middle.astype(F32)).astype(BF16)
    total[...] += contract(
        jnp.concatenate([onehot] * 3, axis=1), jnp.concatenate([high, middle, low], axis=1), 1, 1
    )

    @pl.when(i == pl.num_programs(0) - 1)
    def _():
        send_ref[...] = total[...].reshape(send_ref.shape)


def sources(tab, got, spectra, base, pts):
    points = spectra.shape[1]
    blocks = got.shape[0]
    capacity = got.shape[2] // 8
    return pl.pallas_call(
        source_kernel,
        grid=(points // TW,),
        in_specs=[
            pl.BlockSpec(tab.shape, lambda i: (0, 0, 0), pipeline_mode=pl.Buffered(1)),
            pl.BlockSpec(got.shape, lambda i: (0, 0, 0), pipeline_mode=pl.Buffered(1)),
            pl.BlockSpec((K, TW), lambda i: (0, i)),
            pl.BlockSpec((K, TW), lambda i: (0, i)),
            pl.BlockSpec((8, TW), lambda i: (0, i)),
        ],
        out_specs=[
            pl.BlockSpec((K, TW), lambda i: (0, i)),
            pl.BlockSpec((blocks, 1, 4 * capacity), lambda i: (0, 0, 0)),
        ],
        out_shape=[
            jax.ShapeDtypeStruct((K, points), BF16),
            jax.ShapeDtypeStruct((blocks, 1, 4 * capacity), F32),
        ],
        scratch_shapes=[
            pltpu.VMEM((2 * capacity, blocks), BF16),
            pltpu.VMEM((blocks, 4 * capacity), F32),
        ],
        compiler_params=params(32),
        cost_estimate=cost(10 * K * points, K * points * 8),
        name="sources",
    )(tab, got, spectra, base, pts)


def move_kernel(
    tab_ref, got_ref, own_ref, bh_ref, sb_ref, sa_ref, pb_ref, pa_ref, link_ref, p_ref,
    out_ref, table, natural, south_rows, north_rows, south_y, north_y,
):
    q = pl.program_id(0)
    halo = H // TW
    tiles = pl.num_programs(0)
    lag = 2 * halo
    mine = pl.ds(pl.multiple_of(q * TW, TW), TW)

    @pl.when(q == 0)
    def _():
        got = got_ref[...].reshape(got_ref.shape[0], got_ref.shape[2])
        table[...] = got.T.astype(BF16)

    def keep(m, x):
        natural[m * CH : (m + 1) * CH, mine] = x.astype(BF16)
        for ref, chosen in ((south_rows, S_TILES), (north_rows, N_TILES)):
            rows = [x[HALF * h + 8 * t : HALF * h + 8 * t + 8] for h in range(2) for t in chosen]
            ref[m * 2 * PICK : (m + 1) * 2 * PICK, mine] = jnp.concatenate(rows, axis=0).astype(BF16)

    def halo_tile(s_ref, pts, shift):
        slots = table.shape[0] // 4
        mask = pts[2:3, :]
        east, north, _, _ = winds_at(table[shift * slots : (shift + 1) * slots, :], pts[0:1, :], pts[1:2, :])
        east, north = east * mask, north * mask
        patterns = [
            growth_pattern(tab_ref, east[:, l * 128 : l * 128 + 128], north[:, l * 128 : l * 128 + 128])
            for l in range(TW // 128)
        ]
        pattern = jnp.concatenate(patterns, axis=1)
        for m in range(NCH):
            s = s_ref[m * CH : (m + 1) * CH, :].astype(F32)
            b = bh_ref[m * CH : (m + 1) * CH, :]
            out = []
            for h in range(2):
                scale = step_scale(m, h)
                half = slice(h * HALF, (h + 1) * HALF)
                out.append(b[half] + scale * (jnp.maximum(pattern - 0.25 / scale, 0.0) * s[half]))
            keep(m, jnp.concatenate(out, axis=0))

    @pl.when(q < halo)
    def _():
        halo_tile(sb_ref, pb_ref[...].astype(F32), 0)

    @pl.when(jnp.logical_and(q >= halo, q < tiles - halo))
    def _():
        for m in range(NCH):
            keep(m, own_ref[m * CH : (m + 1) * CH, :].astype(F32))

    @pl.when(q >= tiles - halo)
    def _():
        halo_tile(sa_ref, pa_ref[...].astype(F32), 2)

    @pl.when(q >= lag)
    def _():
        j = q - lag
        width = TW + H
        first = pl.multiple_of(j * TW, TW)
        second = pl.multiple_of(j * TW + H, TW)
        south_hot = hot(iota((width, TW), 0) == link_ref[2:3, :] - first)
        south_y[...] = jnp.dot(south_rows[:, pl.ds(first, width)], south_hot, preferred_element_type=F32)
        north_hot = hot(iota((width, TW), 0) == link_ref[3:4, :] - second)
        north_y[...] = jnp.dot(north_rows[:, pl.ds(second, width)], north_hot, preferred_element_type=F32)
        mask = p_ref[2:3, :]
        lane = iota((8, 128), 1)
        for l in range(TW // 128):
            lanes = slice(l * 128, (l + 1) * 128)
            msk = jnp.broadcast_to(mask[:, lanes], (8, 128))
            near = [pl.ds(pl.multiple_of(second + (l + o) * 128, 128), 128) for o in (-1, 0, 1)]
            for m in range(NCH):
                rows = slice(m * CH, (m + 1) * CH)
                left, here, right = (natural[rows, at].astype(F32) for at in near)
                ys = south_y[m * 2 * PICK : (m + 1) * 2 * PICK, lanes]
                yn = north_y[m * 2 * PICK : (m + 1) * 2 * PICK, lanes]
                out = []
                for h in range(2):
                    shrink = 1.1 ** (-(4 * m + 2 * h))
                    for t in range(9):
                        at = HALF * h + 8 * t
                        c = here[at : at + 8]
                        kind = west_kind(t)
                        if kind != "east":
                            west = jnp.where(
                                lane == 0, pltpu.roll(left[at : at + 8], 1, 1), pltpu.roll(c, 1, 1)
                            )
                            x = west
                        if kind != "west":
                            east = jnp.where(
                                lane == 127, pltpu.roll(right[at : at + 8], 127, 1), pltpu.roll(c, 127, 1)
                            )
                            x = east
                        tr = slice(8 * t, 8 * t + 8)
                        if kind == "both":
                            x = jnp.where(tab_ref[5, tr] > 0, west, east)
                        if t in S_TILES:
                            k = PICK * h + 8 * S_TILES.index(t)
                            y = ys[k : k + 8]
                        if t in N_TILES:
                            k = PICK * h + 8 * N_TILES.index(t)
                            y = jnp.where(tab_ref[6, tr] > 0, y, yn[k : k + 8]) if t in S_TILES else yn[k : k + 8]
                        flow = (tab_ref[2, tr] * x + tab_ref[3, tr] * y) * msk - tab_ref[4, tr] * c
                        out.append(c + shrink * flow)
                out_ref[rows, lanes] = jnp.concatenate(out, axis=0).astype(BF16)


def move(tab, got, own, base_h, before, after, links, pts):
    points = own.shape[1]
    halo = H // TW
    lag = 2 * halo
    mine = points // TW
    steps = mine + lag
    early = lambda q: jnp.minimum(q, halo - 1)
    late = lambda q: jnp.clip(q - mine - halo, 0, halo - 1)
    out_at = lambda q: jnp.clip(q - lag, 0, mine - 1)
    both = lambda q: jnp.where(q < mine + halo, early(q), halo + late(q))
    extended = points + 2 * H
    return pl.pallas_call(
        move_kernel,
        grid=(steps,),
        in_specs=[
            pl.BlockSpec(tab.shape, lambda q: (0, 0, 0), pipeline_mode=pl.Buffered(1)),
            pl.BlockSpec(got.shape, lambda q: (0, 0, 0), pipeline_mode=pl.Buffered(1)),
            pl.BlockSpec((K, TW), lambda q: (0, jnp.clip(q - halo, 0, mine - 1))),
            pl.BlockSpec((K, TW), lambda q: (0, both(q))),
            pl.BlockSpec((K, TW), lambda q: (0, early(q))),
            pl.BlockSpec((K, TW), lambda q: (0, late(q))),
            pl.BlockSpec((16, TW), lambda q: (K // 16, early(q))),
            pl.BlockSpec((16, TW), lambda q: (K // 16, late(q))),
            pl.BlockSpec((4, TW), lambda q: (0, out_at(q))),
            pl.BlockSpec((8, TW), lambda q: (0, out_at(q))),
        ],
        out_specs=pl.BlockSpec((K, TW), lambda q: (0, out_at(q))),
        out_shape=jax.ShapeDtypeStruct((K, points), BF16),
        scratch_shapes=[
            pltpu.VMEM((got.shape[2], got.shape[0]), BF16),
            pltpu.VMEM((K, extended), BF16),
            pltpu.VMEM((18 * PICK, extended), BF16),
            pltpu.VMEM((18 * PICK, extended), BF16),
            pltpu.VMEM((18 * PICK, TW), F32),
            pltpu.VMEM((18 * PICK, TW), F32),
        ],
        compiler_params=params(48),
        cost_estimate=cost(2 * 2 * 18 * PICK * (TW + H) * points, K * points * 8),
        name="move",
    )(tab, got, own, base_h, before, after, before, after, links, pts)


def cell_kernel(got_ref, push_ref, pusht_ref, air_ref, wind_ref, rough_ref, left, right):
    capacity, blocks = pusht_ref.shape
    lat_dev = air_ref.shape[1]
    values = got_ref[...].reshape(blocks, 4 * capacity).T
    high = values.astype(BF16).astype(F32)
    low = values - high
    for r in range(capacity):
        cols = slice(r * blocks, (r + 1) * blocks)
        at_row = iota((lat_dev, blocks), 0) == (pusht_ref[r : r + 1, :] >> 7)
        for part, source in enumerate((high, low)):
            rows = [
                jnp.where(at_row, source[c * capacity + r : c * capacity + r + 1, :], 0.0) for c in range(4)
            ]
            left[part * 4 * lat_dev : (part + 1) * 4 * lat_dev, cols] = jnp.concatenate(rows, axis=0).astype(BF16)
        right[cols, :] = hot(iota((blocks, 128), 1) == (push_ref[:, r : r + 1] & 127))
    sums = jnp.dot(left[...], right[...], preferred_element_type=F32)
    sums = sums[: 4 * lat_dev] + sums[4 * lat_dev :]
    sx, sy, rough, share = (sums[c * lat_dev : (c + 1) * lat_dev] for c in range(4))
    count = jnp.maximum(share, 1.0)
    wind_ref[0] = air_ref[0] - 0.5 * (sx / count)
    wind_ref[1] = air_ref[1] - 0.5 * (sy / count)
    rough_ref[...] = rough / count


def cells(got, push, pusht, air_state):
    capacity, blocks = pusht.shape
    lat_dev = air_state.shape[1]
    return pl.pallas_call(
        cell_kernel,
        out_shape=[
            jax.ShapeDtypeStruct(air_state.shape, F32),
            jax.ShapeDtypeStruct(air_state.shape[1:], F32),
        ],
        scratch_shapes=[
            pltpu.VMEM((8 * lat_dev, capacity * blocks), BF16),
            pltpu.VMEM((capacity * blocks, 128), BF16),
        ],
        compiler_params=params(24),
        cost_estimate=cost(2 * 8 * lat_dev * 128 * capacity * blocks, 400000),
        name="cells",
    )(got, push, pusht, air_state)


def chain(axis, step):
    peers = lax.axis_size(axis)
    pairs = [(i, i + 1) for i in range(peers - 1)]
    return pairs if step > 0 else [(j, i) for i, j in pairs]


def shards(spectra, interact, sea_mask, sea_tile, push_list, neighbors, air_wind, diffusion):
    both = ("wave", "atm")
    tab = jnp.asarray(row_tables())
    lat_total = air_wind.shape[1] * lax.axis_size("atm")
    points = spectra.shape[1]
    push = push_list[0]

    pack = jnp.concatenate([air_wind, diffusion[None]], axis=0)
    above = lax.ppermute(pack[:, -8:], "atm", chain("atm", 1))
    below = lax.ppermute(pack[:, :8], "atm", chain("atm", -1))
    mid = jnp.concatenate([above, pack, below], axis=1)
    left = lax.ppermute(mid, "wave", chain("wave", 1))
    right = lax.ppermute(mid, "wave", chain("wave", -1))

    pts, pusht, to_prev, to_next = prepare(
        sea_tile.reshape(1, points), sea_mask.reshape(1, points), push, spectra
    )
    before = lax.ppermute(to_next, both, chain(both, 1))
    after = lax.ppermute(to_prev, both, chain(both, -1))

    air_state, outgoing = air(lat_total, mid, left, right, pusht)
    arrived = lax.all_to_all(outgoing, both, split_axis=0, concat_axis=0, tiled=True)

    base = base_own(interact, spectra, pts)
    base_h = base_halo(interact, before, after)
    sourced, outbound = sources(tab, arrived, spectra, base, pts)
    inbound = lax.all_to_all(outbound, both, split_axis=0, concat_axis=0, tiled=True)
    wave_spectra = move(tab, arrived, sourced, base_h, before, after, neighbors, pts)
    surface_wind, roughness = cells(inbound, push, pusht, air_state)
    return (wave_spectra, surface_wind, roughness)


def solution(mesh):
    placed = (
        P(None, ("wave", "atm")),
        P(),
        P(("wave", "atm")),
        P(("wave", "atm")),
        P(("wave", "atm"), None, None),
        P(None, ("wave", "atm")),
        P(None, "atm", "wave"),
        P("atm", "wave"),
    )
    return jax.shard_map(
        shards,
        mesh=mesh,
        in_specs=placed,
        out_specs=(P(None, ("wave", "atm")), P(None, "atm", "wave"), P("atm", "wave")),
        check_vma=False,
    )
```

profile of v0, /device:TPU:1, one launch (start us, length us, event | category | flops | bytes accessed | tf_op | source)
XLA Modules:
  0.0 138.9 jit_solution(193588014220903788)
XLA Ops:
  1.5 2.5 %copy-done = bf16[1296,2048]{1,0:T(8,128)(2,1)S(1)} copy-done((bf16[1296,2048]{1,0:T(8,128)(2,1)S(1)}, bf16[1296,2048]{1,0:T(8,128)(2,1)}, u32[]{:S(2)}) %copy-start) | copy-done | bytes 5308440
  5.4 2.0 %prepare.1 = (f32[8,2048]{1,0:T(8,128)S(1)}, s32[32,128]{1,0:T(8,128)S(1)}, bf16[1312,512]{1,0:T(8,128)(2,1)}, bf16[1312,512]{1,0:T(8,128)(2,1)}) custom-call(s32[1,2048]{1,0:T(1,128)S(1)} %bitcast.6, s32[1,2048]{1,0:T(1,128)S(1)} %bitcast.7, s32[128,32]{1,0:T(8,128)S(1)} %bitcast.4, bf16[1296,2048]{1,0:T(8,128)(2,1)S(1)} %copy-done, ...), custom_call_target="tpu_custom_call" | custom-call | flops 268435456 | bytes 5373952 | tf_op jit(solution)/shard_map/prepare/pallas_call | solution.py:108
  7.4 4.9 %collective-permute-start.4 = (bf16[1312,512]{1,0:T(8,128)(2,1)}, bf16[1312,512]{1,0:T(8,128)(2,1)S(1)}, u32[]{:S(2)}, u32[]{:S(2)}) collective-permute-start(bf16[1312,512]{1,0:T(8,128)(2,1)} %get-tuple-element.17), channel_id=1, source_target_pairs={{0,1},{1,2},{2,3},{3,4},{4,5},{5,6},{6,7},{7,8},{8,9},{9,10},{10,1... | collective-permute-start | bytes 4030472 | tf_op jit(solution)/shard_map/ppermute | solution.py:591
  12.3 1.9 %collective-permute-start.5 = (bf16[1312,512]{1,0:T(8,128)(2,1)}, bf16[1312,512]{1,0:T(8,128)(2,1)S(1)}, u32[]{:S(2)}, u32[]{:S(2)}) collective-permute-start(bf16[1312,512]{1,0:T(8,128)(2,1)} %get-tuple-element.18), channel_id=1, source_target_pairs={{1,0},{2,1},{3,2},{4,3},{5,4},{6,5},{7,6},{8,7},{9,8},{10,9},{11,1... | collective-permute-start | bytes 4030472 | tf_op jit(solution)/shard_map/ppermute | solution.py:592
  14.3 3.6 %collective-permute-start = (f32[3,8,128]{2,1,0:T(8,128)S(1)}, f32[3,8,128]{2,1,0:T(8,128)S(1)}, u32[]{:S(2)}, u32[]{:S(2)}) collective-permute-start(f32[3,8,128]{2,1,0:T(8,128)S(1)} %get-tuple-element.23), channel_id=1, source_target_pairs={{0,1},{1,2},{2,3},{3,4},{4,5},{5,6},{6,7},{8,9},{9,10},{10,11},{11... | collective-permute-start | bytes 36872 | tf_op jit(solution)/shard_map/ppermute | solution.py:582
  17.9 1.9 %collective-permute-start.1 = (f32[3,8,128]{2,1,0:T(8,128)S(1)}, f32[3,8,128]{2,1,0:T(8,128)S(1)}, u32[]{:S(2)}, u32[]{:S(2)}) collective-permute-start(f32[3,8,128]{2,1,0:T(8,128)S(1)} %get-tuple-element.24), channel_id=1, source_target_pairs={{1,0},{2,1},{3,2},{4,3},{5,4},{6,5},{7,6},{9,8},{10,9},{11,10},{12... | collective-permute-start | bytes 36872 | tf_op jit(solution)/shard_map/ppermute | solution.py:583
  19.8 7.7 %collective-permute-done = f32[3,8,128]{2,1,0:T(8,128)S(1)} collective-permute-done((f32[3,8,128]{2,1,0:T(8,128)S(1)}, f32[3,8,128]{2,1,0:T(8,128)S(1)}, u32[]{:S(2)}, u32[]{:S(2)}) %collective-permute-start) | collective-permute-done | bytes 12320 | tf_op jit(solution)/shard_map/ppermute | solution.py:582
  27.5 4.4 %collective-permute-done.1 = f32[3,8,128]{2,1,0:T(8,128)S(1)} collective-permute-done((f32[3,8,128]{2,1,0:T(8,128)S(1)}, f32[3,8,128]{2,1,0:T(8,128)S(1)}, u32[]{:S(2)}, u32[]{:S(2)}) %collective-permute-start.1) | collective-permute-done | bytes 12320 | tf_op jit(solution)/shard_map/ppermute | solution.py:583
  31.9 3.1 %collective-permute-start.2 = (f32[3,80,128]{2,1,0:T(8,128)S(1)}, f32[3,80,128]{2,1,0:T(8,128)S(1)}, u32[]{:S(2)}, u32[]{:S(2)}) collective-permute-start(f32[3,80,128]{2,1,0:T(8,128)S(1)} %pad_maximum_fusion.refs_0_), channel_id=1, source_target_pairs={{0,8},{8,16},{16,24},{24,32},{32,40},{40,48},{48,56},{56,64},{64,7... | collective-permute-start | bytes 368648 | tf_op jit(solution)/shard_map/ppermute | solution.py:585
  36.9 3.8 %collective-permute-done.3.refs_2_ = f32[3,80,128]{2,1,0:T(8,128)S(1)} collective-permute-done((f32[3,80,128]{2,1,0:T(8,128)S(1)}, f32[3,80,128]{2,1,0:T(8,128)S(1)}, u32[]{:S(2)}, u32[]{:S(2)}) %collective-permute-start.3) | collective-permute-done | bytes 122912 | tf_op jit(solution)/shard_map/ppermute | solution.py:586
  40.7 2.2 %air.1 = (f32[2,64,128]{2,1,0:T(8,128)S(1)}, f32[128,1,256]{2,1,0:T(1,128)}) custom-call(f32[3,80,128]{2,1,0:T(8,128)S(1)} %pad_maximum_fusion.refs_0_, f32[3,80,128]{2,1,0:T(8,128)S(1)} %collective-permute-done.2.refs_1_, f32[3,80,128]{2,1,0:T(8,128)S(1)} %collective-permute-done.3.refs_2_, s32[32,128]{1,0:T(8,128)S(1)} %get-tuple-element.13.refs_3_.pusht_ref), custom_call_target="tpu_custom_call" | custom-call | flops 134217728 | bytes 600000 | tf_op jit(solution)/shard_map/air/pallas_call | solution.py:263
  42.8 11.9 %all-to-all-start = ((f32[128,1,256]{2,1,0:T(1,128)}), f32[128,1,256]{2,1,0:T(1,128)S(1)}, u32[]{:S(2)}, u32[]{:S(2)}) async-start(f32[128,1,256]{2,1,0:T(1,128)} %get-tuple-element.14), calls=%async_computation | async-start | bytes 262144 | tf_op jit(solution)/shard_map/all_to_all | solution.py:595
  54.7 2.5 %copy-done.1 = bf16[1296,2048]{1,0:T(8,128)(2,1)S(1)} copy-done((bf16[1296,2048]{1,0:T(8,128)(2,1)S(1)}, bf16[1296,2048]{1,0:T(8,128)(2,1)}, u32[]{:S(2)}) %copy-start.1) | copy-done | bytes 5308440
  57.2 2.0 %copy-done.7 = bf16[1296,1296]{1,0:T(8,128)(2,1)S(1)} copy-done((bf16[1296,1296]{1,0:T(8,128)(2,1)S(1)}, bf16[1296,1296]{1,0:T(8,128)(2,1)}, u32[]{:S(2)}) %copy-start.7) | copy-done | bytes 3359256
  59.3 11.3 %base_own.1.base_ref = f32[1296,2048]{1,0:T(8,128)S(1)} custom-call(bf16[1296,1296]{1,0:T(8,128)(2,1)S(1)} %copy-done.7, bf16[1296,2048]{1,0:T(8,128)(2,1)S(1)} %copy-done.1, f32[8,2048]{1,0:T(8,128)S(1)} %get-tuple-element.15.p_ref), custom_call_target="tpu_custom_call" | custom-call | flops 6879707136 | bytes 19284480 | tf_op jit(solution)/shard_map/base_own/pallas_call | solution.py:165
  70.6 4.0 %copy-done.4 = f32[1296,2048]{1,0:T(8,128)} copy-done((f32[1296,2048]{1,0:T(8,128)}, f32[1296,2048]{1,0:T(8,128)S(1)}, u32[]{:S(2)}) %copy-start.4) | copy-done | bytes 10616856
  74.7 2.5 %copy-done.2 = bf16[1296,2048]{1,0:T(8,128)(2,1)S(1)} copy-done((bf16[1296,2048]{1,0:T(8,128)(2,1)S(1)}, bf16[1296,2048]{1,0:T(8,128)(2,1)}, u32[]{:S(2)}) %copy-start.2) | copy-done | bytes 5308440
  77.2 4.0 %copy-done.5 = f32[1296,2048]{1,0:T(8,128)S(1)} copy-done((f32[1296,2048]{1,0:T(8,128)S(1)}, f32[1296,2048]{1,0:T(8,128)}, u32[]{:S(2)}) %copy-start.5) | copy-done | bytes 10616856
  81.2 9.1 %sources.1 = (bf16[1296,2048]{1,0:T(8,128)(2,1)S(1)}, f32[128,1,128]{2,1,0:T(1,128)S(1)}) custom-call(f32[7,72,128]{2,1,0:T(8,128)S(1)} %copy-done.9, f32[128,1,256]{2,1,0:T(1,128)S(1)} %all-to-all-done.got_ref, bf16[1296,2048]{1,0:T(8,128)(2,1)S(1)} %copy-done.2, f32[1296,2048]{1,0:T(8,128)S(1)} %copy-done.5, f32[8,2048]{1,0:T(8,128)S(1)} %get-tuple-element.15.p_ref), custom_call_target="tpu_custom_call" | custom-call | flops 26542080 | bytes 21233664 | tf_op jit(solution)/shard_map/sources/pallas_call | solution.py:349
  90.3 19.0 %all_to_all.10.got_ref = f32[128,1,128]{2,1,0:T(1,128)S(1)} all-to-all(f32[128,1,128]{2,1,0:T(1,128)S(1)} %get-tuple-element.19), channel_id=1, replica_groups=mesh['wave'=16,'atm'=8] {'wave','atm'}, dimensions={0} | all-to-all | bytes 131072 | tf_op jit(solution)/shard_map/all_to_all | solution.py:600
  109.3 2.5 %cells.1 = (f32[2,64,128]{2,1,0:T(8,128)}, f32[64,128]{1,0:T(8,128)}) custom-call(f32[128,1,128]{2,1,0:T(1,128)S(1)} %all_to_all.10.got_ref, s32[128,32]{1,0:T(8,128)S(1)} %bitcast.5, s32[32,128]{1,0:T(8,128)S(1)} %get-tuple-element.13.refs_3_.pusht_ref, f32[2,64,128]{2,1,0:T(8,128)S(1)} %get-tuple-element.20.air_ref), custom_call_target="tpu_custom_call" | custom-call | flops 536870912 | bytes 400000 | tf_op jit(solution)/shard_map/cells/pallas_call | solution.py:552
  111.8 5.7 %base_halo.1.bh_ref = f32[1296,1024]{1,0:T(8,128)S(1)} custom-call(bf16[1296,1296]{1,0:T(8,128)(2,1)S(1)} %copy-done.8, bf16[1312,512]{1,0:T(8,128)(2,1)S(1)} %collective-permute-done.4.sb_ref.pb_ref, bf16[1312,512]{1,0:T(8,128)(2,1)S(1)} %collective-permute-done.5.sa_ref.pa_ref, bf16[1312,512]{1,0:T(8,128)(2,1)S(1)} %collective-permute-done.4.sb_ref.pb_ref, ...), custom_call_target="tpu_custom_call" | custom-call | flops 3439853568 | bytes 11321856 | tf_op jit(solution)/shard_map/base_halo/pallas_call | solution.py:197
  117.5 2.4 %copy-done.3 = f32[1296,1024]{1,0:T(8,128)} copy-done((f32[1296,1024]{1,0:T(8,128)}, f32[1296,1024]{1,0:T(8,128)S(1)}, u32[]{:S(2)}) %copy-start.3) | copy-done | bytes 5308440
  119.9 19.0 %move.1 = bf16[1296,2048]{1,0:T(8,128)(2,1)} custom-call(f32[7,72,128]{2,1,0:T(8,128)S(1)} %copy-done.9, f32[128,1,256]{2,1,0:T(1,128)S(1)} %all-to-all-done.got_ref, bf16[1296,2048]{1,0:T(8,128)(2,1)} %copy-done.6, f32[1296,1024]{1,0:T(8,128)} %copy-done.3, bf16[1312,512]{1,0:T(8,128)(2,1)S(1)} %collective-permute-done.4.sb_ref.pb_ref, ...), custom_call_target="tpu_custom_call" | custom-call | flops 5435817984 | bytes 21233664 | tf_op jit(solution)/shard_map/move/pallas_call | solution.py:494
  (31 shorter events, 4.1 us)
Async XLA Ops:
  1.4 2.5 %copy-start = (bf16[1296,2048]{1,0:T(8,128)(2,1)S(1)}, bf16[1296,2048]{1,0:T(8,128)(2,1)}, u32[]{:S(2)}) copy-start(bf16[1296,2048]{1,0:T(8,128)(2,1)} %s_ref.3) | copy-start | bytes 15925252
  4.0 0.7 copy-start.11
  4.7 0.7 copy-start.12
  5.3 8.9 %copy-start.13 = (f32[2,64,128]{2,1,0:T(8,128)S(1)}, f32[2,64,128]{2,1,0:T(8,128)}, u32[]{:S(2)}) copy-start(f32[2,64,128]{2,1,0:T(8,128)} %param.15) | copy-start | bytes 196612
  5.4 8.9 %copy-start.14 = (f32[64,128]{1,0:T(8,128)S(1)}, f32[64,128]{1,0:T(8,128)}, u32[]{:S(2)}) copy-start(f32[64,128]{1,0:T(8,128)} %param.16) | copy-start | bytes 98308
  7.4 104.4 %collective-permute-start.4 = (bf16[1312,512]{1,0:T(8,128)(2,1)}, bf16[1312,512]{1,0:T(8,128)(2,1)S(1)}, u32[]{:S(2)}, u32[]{:S(2)}) collective-permute-start(bf16[1312,512]{1,0:T(8,128)(2,1)} %get-tuple-element.17), channel_id=1, source_target_pairs={{0,1},{1,2},{2,3},{3,4},{4,5},{5,6},{6,7},{7,8},{8,9},{9,10},{10,1... | collective-permute-start | bytes 4030472 | tf_op jit(solution)/shard_map/ppermute | solution.py:591
  12.3 99.5 %collective-permute-start.5 = (bf16[1312,512]{1,0:T(8,128)(2,1)}, bf16[1312,512]{1,0:T(8,128)(2,1)S(1)}, u32[]{:S(2)}, u32[]{:S(2)}) collective-permute-start(bf16[1312,512]{1,0:T(8,128)(2,1)} %get-tuple-element.18), channel_id=1, source_target_pairs={{1,0},{2,1},{3,2},{4,3},{5,4},{6,5},{7,6},{8,7},{9,8},{10,9},{11,1... | collective-permute-start | bytes 4030472 | tf_op jit(solution)/shard_map/ppermute | solution.py:592
  14.3 13.3 %collective-permute-start = (f32[3,8,128]{2,1,0:T(8,128)S(1)}, f32[3,8,128]{2,1,0:T(8,128)S(1)}, u32[]{:S(2)}, u32[]{:S(2)}) collective-permute-start(f32[3,8,128]{2,1,0:T(8,128)S(1)} %get-tuple-element.23), channel_id=1, source_target_pairs={{0,1},{1,2},{2,3},{3,4},{4,5},{5,6},{6,7},{8,9},{9,10},{10,11},{11... | collective-permute-start | bytes 36872 | tf_op jit(solution)/shard_map/ppermute | solution.py:582
  17.9 14.0 %collective-permute-start.1 = (f32[3,8,128]{2,1,0:T(8,128)S(1)}, f32[3,8,128]{2,1,0:T(8,128)S(1)}, u32[]{:S(2)}, u32[]{:S(2)}) collective-permute-start(f32[3,8,128]{2,1,0:T(8,128)S(1)} %get-tuple-element.24), channel_id=1, source_target_pairs={{1,0},{2,1},{3,2},{4,3},{5,4},{6,5},{7,6},{9,8},{10,9},{11,10},{12... | collective-permute-start | bytes 36872 | tf_op jit(solution)/shard_map/ppermute | solution.py:583
  31.9 5.0 %collective-permute-start.2 = (f32[3,80,128]{2,1,0:T(8,128)S(1)}, f32[3,80,128]{2,1,0:T(8,128)S(1)}, u32[]{:S(2)}, u32[]{:S(2)}) collective-permute-start(f32[3,80,128]{2,1,0:T(8,128)S(1)} %pad_maximum_fusion.refs_0_), channel_id=1, source_target_pairs={{0,8},{8,16},{16,24},{24,32},{32,40},{40,48},{48,56},{56,64},{64,7... | collective-permute-start | bytes 368648 | tf_op jit(solution)/shard_map/ppermute | solution.py:585
  35.1 5.6 %collective-permute-start.3 = (f32[3,80,128]{2,1,0:T(8,128)S(1)}, f32[3,80,128]{2,1,0:T(8,128)S(1)}, u32[]{:S(2)}, u32[]{:S(2)}) collective-permute-start(f32[3,80,128]{2,1,0:T(8,128)S(1)} %pad_maximum_fusion.refs_0_), channel_id=1, source_target_pairs={{8,0},{16,8},{24,16},{32,24},{40,32},{48,40},{56,48},{64,56},{72,6... | collective-permute-start | bytes 368648 | tf_op jit(solution)/shard_map/ppermute | solution.py:586
  42.8 31.8 %all-to-all-start = ((f32[128,1,256]{2,1,0:T(1,128)}), f32[128,1,256]{2,1,0:T(1,128)S(1)}, u32[]{:S(2)}, u32[]{:S(2)}) async-start(f32[128,1,256]{2,1,0:T(1,128)} %get-tuple-element.14), calls=%async_computation | async-start | bytes 262144 | tf_op jit(solution)/shard_map/all_to_all | solution.py:595
  54.7 2.5 %copy-start.1 = (bf16[1296,2048]{1,0:T(8,128)(2,1)S(1)}, bf16[1296,2048]{1,0:T(8,128)(2,1)}, u32[]{:S(2)}) copy-start(bf16[1296,2048]{1,0:T(8,128)(2,1)} %s_ref.3) | copy-start | bytes 15925252
  57.2 2.0 %copy-start.7 = (bf16[1296,1296]{1,0:T(8,128)(2,1)S(1)}, bf16[1296,1296]{1,0:T(8,128)(2,1)}, u32[]{:S(2)}) copy-start(bf16[1296,1296]{1,0:T(8,128)(2,1)} %it_ref.3) | copy-start | bytes 10077700
  59.3 15.4 %copy-start.9 = (f32[7,72,128]{2,1,0:T(8,128)S(1)}, f32[7,72,128]{2,1,0:T(8,128)}, u32[]{:S(2)}) copy-start(f32[7,72,128]{2,1,0:T(8,128)} %constant.2.clone.tab_ref) | copy-start | bytes 774148
  70.6 4.1 %copy-start.4 = (f32[1296,2048]{1,0:T(8,128)}, f32[1296,2048]{1,0:T(8,128)S(1)}, u32[]{:S(2)}) copy-start(f32[1296,2048]{1,0:T(8,128)S(1)} %base_own.1.base_ref) | copy-start | bytes 31850500
  74.7 2.5 %copy-start.2 = (bf16[1296,2048]{1,0:T(8,128)(2,1)S(1)}, bf16[1296,2048]{1,0:T(8,128)(2,1)}, u32[]{:S(2)}) copy-start(bf16[1296,2048]{1,0:T(8,128)(2,1)} %s_ref.3) | copy-start | bytes 15925252
  77.2 4.0 %copy-start.5 = (f32[1296,2048]{1,0:T(8,128)S(1)}, f32[1296,2048]{1,0:T(8,128)}, u32[]{:S(2)}) copy-start(f32[1296,2048]{1,0:T(8,128)} %copy-done.4) | copy-start | bytes 31850500
  81.2 30.6 %copy-start.8 = (bf16[1296,1296]{1,0:T(8,128)(2,1)S(1)}, bf16[1296,1296]{1,0:T(8,128)(2,1)}, u32[]{:S(2)}) copy-start(bf16[1296,1296]{1,0:T(8,128)(2,1)} %it_ref.3) | copy-start | bytes 10077700
  90.3 27.2 %copy-start.6 = (bf16[1296,2048]{1,0:T(8,128)(2,1)}, bf16[1296,2048]{1,0:T(8,128)(2,1)S(1)}, u32[]{:S(2)}) copy-start(bf16[1296,2048]{1,0:T(8,128)(2,1)S(1)} %get-tuple-element.16.own_ref) | copy-start | bytes 15925252
  111.8 8.1 %copy-start.10 = (s32[4,2048]{1,0:T(4,128)S(1)}, s32[4,2048]{1,0:T(4,128)}, u32[]{:S(2)}) copy-start(s32[4,2048]{1,0:T(4,128)} %link_ref.1) | copy-start | bytes 98308
  117.5 2.4 %copy-start.3 = (f32[1296,1024]{1,0:T(8,128)}, f32[1296,1024]{1,0:T(8,128)S(1)}, u32[]{:S(2)}) copy-start(f32[1296,1024]{1,0:T(8,128)S(1)} %base_halo.1.bh_ref) | copy-start | bytes 15925252
where the time goes:
time: 140 us; the launch traced here: 139 us
  Pallas kernels  51.8 us (37%)
  starting transfers between devices  28.7 us (20%)
  local copies, waits for them, and re-layouts  22.2 us (16%)
  blocking collectives  19 us (14%)
  waiting for transfers between devices  16.4 us (12%)
    unnamed x31, local copies, waits for them, and re-layouts  22.2 us
    pallas_call x1, Pallas kernels, move(): pl.pallas_call(move_kernel, grid=(steps,), in_specs=[pl.BlockSpec(tab.sha...  19 us
    all_to_all x1, blocking collectives, shards(): lax.all_to_all(outbound, both, split_axis=0, concat_axis=0, tiled=True)  19 us
    all_to_all x1, starting transfers between devices, shards(): lax.all_to_all(outgoing, both, split_axis=0, concat_axis=0, tiled=True)  11.9 us
    pallas_call x1, Pallas kernels, base_own(): pl.pallas_call(base_kernel, grid=(points // TW,), in_specs=[pl.BlockSpec(...  11.3 us
    pallas_call x1, Pallas kernels, sources(): pl.pallas_call(source_kernel, grid=(points // TW,), in_specs=[pl.BlockSpe...  9.12 us
    ppermute x1, waiting for transfers between devices, shards(): above = lax.ppermute(pack[:, -8:], 'atm', chain('atm', 1))  7.69 us
    pallas_call x1, Pallas kernels, base_halo(): pl.pallas_call(base_halo_kernel, grid=(2 * n,), in_specs=[pl.BlockSpec((K...  5.69 us
  transfers between devices with their start and end apart: 7, of which 4 were waited for; matrix products, arithmetic and copies ran while one was open for 0% of the time, Pallas kernels for 18%

commit v1 on v0

v1 whole, which is shorter than its diff:
```python
import math

import jax
import jax.numpy as jnp
import numpy as np
from jax import lax
from jax.experimental import pallas as pl
from jax.experimental.pallas import tpu as pltpu
from jax.sharding import PartitionSpec as P

ND = 36
NF = 36
K = ND * NF
H = 512
ATM_STEPS = 4
TW = 256
CH = 144
NCH = K // CH
HALF = 72
HALO_ROWS = K + 16
F32 = jnp.float32
BF16 = jnp.bfloat16
I32 = jnp.int32

S_TILES = (0, 1, 2, 4, 5, 6)
N_TILES = (2, 3, 4, 6, 7, 8)
PICK = 8 * len(S_TILES)


def row_tables():
    r = np.arange(HALF)
    d = r % ND
    angle = (d + 0.5) * (2.0 * math.pi / ND)
    up = np.power(1.1, r // ND)
    cosine, sine = np.cos(angle), np.sin(angle)
    reach = 0.7 / up
    rows = [
        up * cosine,
        up * sine,
        np.abs(reach * cosine),
        np.abs(reach * sine),
        np.abs(reach * cosine) + np.abs(reach * sine),
        (cosine > 0).astype(np.float64),
        (sine > 0).astype(np.float64),
    ]
    table = np.stack(rows).astype(np.float32)
    return np.ascontiguousarray(np.broadcast_to(table[:, :, None], table.shape + (128,)))


COS_POS = [bool(math.cos((d + 0.5) * 2.0 * math.pi / ND) > 0) for d in range(ND)]


def west_kind(tile):
    signs = {COS_POS[(8 * tile + s) % ND] for s in range(8)}
    return "both" if len(signs) == 2 else ("west" if True in signs else "east")


def iota(shape, dim):
    return lax.broadcasted_iota(I32, shape, dim)


def hot(mask):
    return jnp.where(mask, 1.0, 0.0).astype(BF16)


def contract(a, b, da, db):
    return lax.dot_general(a, b, (((da,), (db,)), ((), ())), preferred_element_type=F32)


def params(megabytes):
    return pltpu.CompilerParams(vmem_limit_bytes=megabytes << 20)


BIG = 52


HERE = pl.BlockSpec(memory_space=pltpu.VMEM)
AWAY = pl.BlockSpec(memory_space=pl.ANY)


def cost(flops, data):
    return pl.CostEstimate(flops=flops, bytes_accessed=data, transcendentals=0)


def prepare_kernel(tile_ref, mask_ref, push_ref, s_ref, pts_ref, pusht_ref, to_prev, to_next, rims, sems):
    blocks = push_ref.shape[0]
    points = tile_ref.shape[1]
    ends = ((to_prev, 0), (to_next, points - H))
    loads = [
        pltpu.make_async_copy(s_ref.at[:, pl.ds(lo, H)], rims.at[k, pl.ds(0, K), :], sems.at[k])
        for k, (out, lo) in enumerate(ends)
    ]
    for load in loads:
        load.start()
    pusht_ref[...] = push_ref[...].astype(F32).T.astype(I32)
    before = hot(iota((TW, TW), 0) < iota((TW, TW), 1))
    ones = jnp.ones((TW, TW), BF16)
    running = jnp.zeros((blocks, TW), F32)
    for c in range(points // TW):
        cols = slice(c * TW, (c + 1) * TW)
        tile = tile_ref[:, cols]
        same = iota((blocks, TW), 0) == tile
        onehot = hot(same)
        earlier = contract(onehot, before, 1, 0) + running
        rank = jnp.sum(jnp.where(same, earlier, 0.0), axis=0, keepdims=True)
        running = running + contract(onehot, ones, 1, 0)
        pts_ref[0:1, cols] = tile.astype(F32)
        pts_ref[1:2, cols] = rank
        pts_ref[2:3, cols] = mask_ref[:, cols].astype(F32)
        pts_ref[3:8, cols] = jnp.zeros((5, TW), F32)
    stores = []
    for k, (out, lo) in enumerate(ends):
        rows = jnp.concatenate([pts_ref[:, lo : lo + H], jnp.zeros((8, H), F32)], axis=0)
        rims[k, K:, :] = rows.astype(BF16)
        loads[k].wait()
        store = pltpu.make_async_copy(rims.at[k], out, sems.at[2 + k])
        store.start()
        stores.append(store)
    for store in stores:
        store.wait()


def prepare(tile, mask, push, spectra):
    blocks, capacity = push.shape
    points = tile.shape[1]
    return pl.pallas_call(
        prepare_kernel,
        in_specs=[HERE, HERE, HERE, AWAY],
        out_specs=[HERE, HERE, AWAY, AWAY],
        out_shape=[
            jax.ShapeDtypeStruct((8, points), F32),
            jax.ShapeDtypeStruct((capacity, blocks), I32),
            jax.ShapeDtypeStruct((HALO_ROWS, H), BF16),
            jax.ShapeDtypeStruct((HALO_ROWS, H), BF16),
        ],
        scratch_shapes=[pltpu.VMEM((2, HALO_ROWS, H), BF16), pltpu.SemaphoreType.DMA((4,))],
        compiler_params=params(BIG),
        cost_estimate=cost(2 * 2 * blocks * TW * points, 4 * HALO_ROWS * H * 2),
        name="prepare",
    )(tile, mask, push, spectra)


def base_tile(it_ref, s_ref, mask, out_ref, parts):
    depth = K // 3

    def multiply(c):
        rows = slice(c * depth, (c + 1) * depth)
        parts[rows, :] = jnp.dot(it_ref[rows, :], s_ref[...], preferred_element_type=F32)

    multiply(0)
    acc = jnp.zeros((HALF, TW), F32)
    for m in range(NCH):
        s = s_ref[m * CH : (m + 1) * CH, :].astype(F32)
        acc = acc + (s[:HALF] + s[HALF:])
    mean = jnp.sum(acc, axis=0, keepdims=True) * (1.0 / K)
    msk = jnp.broadcast_to(mask, (8, TW))
    quota = jnp.broadcast_to(mean / (1.0 + mean), (8, TW)) * msk * 0.15
    half = 0.5 * msk
    low = iota((8, TW), 0) < 4
    for c in range(3):
        if c < 2:
            multiply(c + 1)
        for m in range(3 * c, 3 * c + 3):
            rows = slice(m * CH, (m + 1) * CH)
            s = s_ref[rows, :].astype(F32)
            n = parts[rows, :]
            keeps = []
            for h in range(2):
                power = 1.21 ** (4 * m + 2 * h - NF / 2)
                a = msk - power * quota
                b = msk - (1.21 * power) * quota
                keeps += [a] * 4 + [jnp.where(low, a, b)] + [b] * 4
            out = [
                s[8 * i : 8 * i + 8] * keep + n[8 * i : 8 * i + 8] * half for i, keep in enumerate(keeps)
            ]
            out_ref[rows, :] = jnp.concatenate(out, axis=0)


def base_kernel(it_ref, s_ref, mask_ref, wait_ref, out_ref, parts):
    base_tile(it_ref, s_ref, mask_ref[...].astype(F32), out_ref, parts)


def base_own(interact, spectra, mask, first, count, wait):
    return pl.pallas_call(
        base_kernel,
        grid=(count,),
        in_specs=[
            pl.BlockSpec((K, K), lambda i: (0, 0), pipeline_mode=pl.Buffered(1)),
            pl.BlockSpec((K, TW), lambda i: (0, i + first)),
            pl.BlockSpec((1, TW), lambda i: (0, i + first)),
            AWAY,
        ],
        out_specs=pl.BlockSpec((K, TW), lambda i: (0, i)),
        out_shape=jax.ShapeDtypeStruct((K, count * TW), F32),
        scratch_shapes=[pltpu.VMEM((K, TW), F32)],
        compiler_params=params(BIG),
        cost_estimate=cost(2 * K * K * count * TW, K * K * 2),
        name="base_own",
    )(interact, spectra, mask, wait)


def base_halo_kernel(it_ref, sb_ref, sa_ref, pb_ref, pa_ref, wait_ref, out_ref, parts):
    i = pl.program_id(0)

    @pl.when(i < H // TW)
    def _():
        base_tile(it_ref, sb_ref, pb_ref[...].astype(F32)[2:3, :], out_ref, parts)

    @pl.when(i >= H // TW)
    def _():
        base_tile(it_ref, sa_ref, pa_ref[...].astype(F32)[2:3, :], out_ref, parts)


def base_halo(interact, before, after, wait):
    n = H // TW
    early = lambda i: jnp.minimum(i, n - 1)
    late = lambda i: jnp.maximum(i - n, 0)
    return pl.pallas_call(
        base_halo_kernel,
        grid=(2 * n,),
        in_specs=[
            pl.BlockSpec((K, K), lambda i: (0, 0), pipeline_mode=pl.Buffered(1)),
            pl.BlockSpec((K, TW), lambda i: (0, early(i))),
            pl.BlockSpec((K, TW), lambda i: (0, late(i))),
            pl.BlockSpec((16, TW), lambda i: (K // 16, early(i))),
            pl.BlockSpec((16, TW), lambda i: (K // 16, late(i))),
            AWAY,
        ],
        out_specs=pl.BlockSpec((K, TW), lambda i: (0, i)),
        out_shape=jax.ShapeDtypeStruct((K, 2 * H), F32),
        scratch_shapes=[pltpu.VMEM((K, TW), F32)],
        compiler_params=params(BIG),
        cost_estimate=cost(2 * K * K * 2 * H, K * K * 2),
        name="base_halo",
    )(interact, before, after, before, after, wait)


def air_kernel(lat_total, mid_ref, left_ref, right_ref, pusht_ref, air_ref, out_ref, slots):
    rows = mid_ref.shape[1]
    lat_dev = rows - 16
    lane = iota((rows, 128), 1)

    def field(i):
        side = jnp.where(lane < 8, right_ref[i], jnp.where(lane >= 120, left_ref[i], 0.0))
        return jnp.concatenate([mid_ref[i], side], axis=1)

    east, north, spread = field(0), field(1), field(2)
    first = lax.axis_index("atm") * lat_dev - 8
    row = (iota((rows, 256), 0) + first).astype(F32)
    turning = 0.05 + 0.1 * row / lat_total

    def laplace(w):
        around = pltpu.roll(w, rows - 1, 0) + pltpu.roll(w, 1, 0) + pltpu.roll(w, 255, 1) + pltpu.roll(w, 1, 1)
        return around - 4.0 * w

    for _ in range(ATM_STEPS):
        e = east + spread * laplace(east) + turning * north
        n = north + spread * laplace(north) - turning * east
        east, north = e, n
    east = east[8 : 8 + lat_dev, :128]
    north = north[8 : 8 + lat_dev, :128]
    air_ref[0] = east
    air_ref[1] = north
    field_t = jnp.concatenate([east.T, north.T], axis=0).astype(BF16)
    capacity, blocks = pusht_ref.shape
    group = 4
    for g in range(capacity // group):
        cells = jnp.concatenate([pusht_ref[g * group + k : g * group + k + 1, :] for k in range(group)], axis=1)
        at_row = hot(iota((lat_dev, group * blocks), 0) == (cells >> 7))
        picked = jnp.dot(field_t, at_row, preferred_element_type=F32)
        at_col = iota((128, group * blocks), 0) == (cells & 127)
        for c in range(2):
            value = jnp.sum(jnp.where(at_col, picked[c * 128 : (c + 1) * 128], 0.0), axis=0, keepdims=True)
            for k in range(group):
                at = c * capacity + g * group + k
                slots[at : at + 1, :] = value[:, k * blocks : (k + 1) * blocks]
    own = slots[...]
    stacked = jnp.concatenate([pltpu.roll(own, 1, 1), own, pltpu.roll(own, blocks - 1, 1), jnp.zeros_like(own)], axis=0)
    out_ref[...] = stacked.T.reshape(out_ref.shape)


def air(lat_total, mid, left, right, pusht, wait):
    capacity, blocks = pusht.shape
    lat_dev = mid.shape[1] - 16
    assert mid.shape[2] == 128 and blocks == 128
    return pl.pallas_call(
        lambda a, b, c, d, wait, *refs: air_kernel(lat_total, a, b, c, d, *refs),
        in_specs=[HERE] * 4 + [AWAY],
        out_specs=[HERE] * 2,
        out_shape=[
            jax.ShapeDtypeStruct((2, lat_dev, 128), F32),
            jax.ShapeDtypeStruct((blocks, 1, 8 * capacity), F32),
        ],
        scratch_shapes=[pltpu.VMEM((2 * capacity, blocks), F32)],
        compiler_params=params(BIG),
        cost_estimate=cost(2 * 256 * lat_dev * capacity * blocks, 600000),
        name="air",
    )(mid, left, right, pusht, wait)


def winds_at(table, tile, rank):
    slots = table.shape[0] // 2
    tiles = table.shape[1]
    points = tile.shape[1]
    onehot = hot(iota((tiles, points), 0) == tile.astype(I32))
    values = jnp.dot(table, onehot, preferred_element_type=F32)
    at = iota((slots, points), 0) == rank.astype(I32)
    east = jnp.sum(jnp.where(at, values[:slots], 0.0), axis=0, keepdims=True)
    north = jnp.sum(jnp.where(at, values[slots:], 0.0), axis=0, keepdims=True)
    return east, north, onehot, at


def growth_pattern(tab_ref, east, north):
    return tab_ref[0] * (0.2 * east) + tab_ref[1] * (0.2 * north)


def step_scale(m, h):
    return 1.1 ** (4 * m + 2 * h - NF / 2)


SW = 512


def lane_tile(i):
    return pl.ds(pl.multiple_of(i * 128, 128), 128)


def stress_kernel(
    tab_ref, got_ref, p_ref, s_hbm, sb_hbm, sa_hbm, wait_ref, send_ref, winds_ref, s_ref, rim, table, waves, sems
):
    points = p_ref.shape[1]
    blocks = got_ref.shape[0]
    slots = got_ref.shape[2] // 4
    groups = points // SW
    rims = [
        pltpu.make_async_copy(ref.at[pl.ds(K, 16), :], rim.at[k], sems.at[groups + k])
        for k, ref in enumerate((sb_hbm, sa_hbm))
    ]
    loads = [
        pltpu.make_async_copy(s_hbm.at[:, pl.ds(g * SW, SW)], s_ref.at[:, pl.ds(g * SW, SW)], sems.at[g])
        for g in range(groups)
    ]
    for load in rims + loads:
        load.start()
    table[...] = got_ref[...].reshape(blocks, got_ref.shape[2]).T.astype(BF16)
    winds_ref[3:8, :] = jnp.zeros((5, winds_ref.shape[1]), F32)

    def place(shift, pts, first):
        cols = slice(first, first + SW)
        east, north, _, _ = winds_at(table[shift * slots : (shift + 1) * slots, :], pts[0:1], pts[1:2])
        mask = pts[2:3]
        winds_ref[0:1, cols] = east * mask
        winds_ref[1:2, cols] = north * mask
        winds_ref[2:3, cols] = mask

    for load in rims:
        load.wait()
    place(0, rim[0].astype(F32), 0)
    place(2, rim[1].astype(F32), H + points)
    for g in range(groups):
        place(1, p_ref[:, g * SW : (g + 1) * SW], H + g * SW)

    def tile(i, carry):
        at = lane_tile(i + H // 128)
        pattern = growth_pattern(tab_ref, winds_ref[0:1, at], winds_ref[1:2, at])
        acc = jnp.zeros((HALF, 128), F32)
        for m in range(NCH):
            s = s_ref[m * CH : (m + 1) * CH, lane_tile(i)].astype(F32)
            for h in range(2):
                scale = step_scale(m, h)
                bent = jnp.maximum((scale * scale) * pattern - 0.25 * scale, 0.0)
                acc = acc + bent * s[h * HALF : (h + 1) * HALF]
        waves[0:1, lane_tile(i)] = jnp.sum(acc * tab_ref[0], axis=0, keepdims=True)
        waves[1:2, lane_tile(i)] = jnp.sum(acc * tab_ref[1], axis=0, keepdims=True)
        return carry

    per = SW // 128
    for g in range(groups):
        loads[g].wait()
        lax.fori_loop(g * per, (g + 1) * per, tile, 0)

    total = jnp.zeros((blocks, 2 * slots), F32)
    for g in range(groups):
        cols = slice(g * SW, (g + 1) * SW)
        east, north, mask = (winds_ref[k : k + 1, H + g * SW : H + (g + 1) * SW] for k in range(3))
        speed = jnp.sqrt(east * east + north * north + 0.25)
        stress_x = 0.3 * speed * east + mask * (waves[0:1, cols] * (0.4 / K))
        stress_y = 0.3 * speed * north + mask * (waves[1:2, cols] * (0.4 / K))
        rough = mask * 0.2 * jnp.sqrt(stress_x * stress_x + stress_y * stress_y + 0.01)
        onehot = hot(iota((blocks, SW), 0) == p_ref[0:1, cols].astype(I32))
        at = iota((slots // 2, SW), 0) == p_ref[1:2, cols].astype(I32)
        values = jnp.concatenate([jnp.where(at, v, 0.0) for v in (stress_x, stress_y, rough, mask)], axis=0)
        high = values.astype(BF16)
        rest = values - high.astype(F32)
        middle = rest.astype(BF16)
        low = (rest - middle.astype(F32)).astype(BF16)
        total = total + contract(
            jnp.concatenate([onehot] * 3, axis=1), jnp.concatenate([high, middle, low], axis=1), 1, 1
        )
    send_ref[...] = total.reshape(send_ref.shape)


def stresses(tab, got, pts, spectra, before, after, wait):
    points = spectra.shape[1]
    blocks = got.shape[0]
    capacity = got.shape[2] // 8
    return pl.pallas_call(
        stress_kernel,
        in_specs=[HERE] * 3 + [AWAY] * 4,
        out_specs=[HERE] * 2,
        out_shape=[
            jax.ShapeDtypeStruct((blocks, 1, 4 * capacity), F32),
            jax.ShapeDtypeStruct((8, points + 2 * H), F32),
        ],
        scratch_shapes=[
            pltpu.VMEM((K, points), BF16),
            pltpu.VMEM((2, 16, H), BF16),
            pltpu.VMEM((8 * capacity, blocks), BF16),
            pltpu.VMEM((8, points), F32),
            pltpu.SemaphoreType.DMA((points // SW + 2,)),
        ],
        compiler_params=params(BIG),
        cost_estimate=cost(10 * K * points, K * points * 2),
        name="stress",
    )(tab, got, pts, spectra, before, after, wait)


def chosen_rows(x, tiles):
    rows = [x[HALF * h + 8 * t : HALF * h + 8 * t + 8] for h in range(2) for t in tiles]
    return jnp.concatenate(rows, axis=0).astype(BF16)


def move_kernel(
    tab_ref, winds_ref, link_ref, s_hbm, sb_hbm, sa_hbm, b_hbm, bh_hbm,
    out_hbm, token, s_ref, b_ref, natural, south, north, staged, south_y, north_y, flows, sems,
):
    points = link_ref.shape[1]
    parts = points // H + 2
    loads = []
    for g in range(parts):
        to = pl.ds(g * H, H)
        if g == 0:
            pair = (sb_hbm.at[pl.ds(0, K), :], bh_hbm.at[:, pl.ds(0, H)])
        elif g == parts - 1:
            pair = (sa_hbm.at[pl.ds(0, K), :], bh_hbm.at[:, pl.ds(H, H)])
        else:
            own = pl.ds((g - 1) * H, H)
            pair = (s_hbm.at[:, own], b_hbm.at[:, own])
        loads.append(pltpu.make_async_copy(pair[0], s_ref.at[:, to], sems.at[2 * g]))
        loads.append(pltpu.make_async_copy(pair[1], b_ref.at[:, to], sems.at[2 * g + 1]))
    for load in loads:
        load.start()
    token[...] = jnp.zeros_like(token)

    def fill(i, kinds):
        at = lane_tile(i)
        pattern = growth_pattern(tab_ref, winds_ref[0:1, at], winds_ref[1:2, at])
        for m in range(NCH):
            rows = slice(m * CH, (m + 1) * CH)
            s = s_ref[rows, at].astype(F32)
            b = b_ref[rows, at]
            out = []
            for h in range(2):
                scale = step_scale(m, h)
                half = slice(h * HALF, (h + 1) * HALF)
                out.append(b[half] + jnp.maximum(scale * pattern - 0.25, 0.0) * s[half])
            x = jnp.concatenate(out, axis=0)
            natural[rows, at] = x.astype(BF16)
            picks = slice(m * 2 * PICK, (m + 1) * 2 * PICK)
            if "s" in kinds:
                south[picks, at] = chosen_rows(x, S_TILES)
            if "n" in kinds:
                north[picks, lane_tile(i - H // 128)] = chosen_rows(x, N_TILES)

    per = H // 128

    def fill_part(g, kinds):
        def body(i, carry):
            fill(i, kinds)
            return carry

        lax.fori_loop(g * per, (g + 1) * per, body, 0)

    def wait_part(g):
        loads[2 * g].wait()
        loads[2 * g + 1].wait()

    def output(j):
        width = TW + H
        window = pl.ds(pl.multiple_of(j * TW, TW), width)
        mine = pl.ds(pl.multiple_of(j * TW, TW), TW)
        south_hot = hot(iota((width, TW), 0) == link_ref[2:3, mine] - j * TW)
        north_hot = hot(iota((width, TW), 0) == link_ref[3:4, mine] - (j * TW + H))
        south_y[...] = jnp.dot(south[:, window], south_hot, preferred_element_type=F32)
        north_y[...] = jnp.dot(north[:, window], north_hot, preferred_element_type=F32)
        first = j * (TW // 128) + per
        for l in range(TW // 128):
            msk = winds_ref[2:3, lane_tile(first + l)]
            flows[l, 0] = tab_ref[2] * msk
            flows[l, 1] = tab_ref[3] * msk
        lane = iota((8, 128), 1)
        for l in range(TW // 128):
            lanes = slice(l * 128, (l + 1) * 128)
            for m in range(NCH):
                rows = slice(m * CH, (m + 1) * CH)
                left, here, right = (natural[rows, lane_tile(first + l + o)].astype(F32) for o in (-1, 0, 1))
                ys = south_y[m * 2 * PICK : (m + 1) * 2 * PICK, lanes]
                yn = north_y[m * 2 * PICK : (m + 1) * 2 * PICK, lanes]
                out = []
                for h in range(2):
                    shrink = 1.1 ** (-(4 * m + 2 * h))
                    for t in range(9):
                        at = HALF * h + 8 * t
                        c = here[at : at + 8]
                        kind = west_kind(t)
                        if kind != "east":
                            west = jnp.where(lane == 0, pltpu.roll(left[at : at + 8], 1, 1), pltpu.roll(c, 1, 1))
                            x = west
                        if kind != "west":
                            east = jnp.where(lane == 127, pltpu.roll(right[at : at + 8], 127, 1), pltpu.roll(c, 127, 1))
                            x = east
                        tr = slice(8 * t, 8 * t + 8)
                        if kind == "both":
                            x = jnp.where(tab_ref[5, tr] > 0, west, east)
                        if t in S_TILES:
                            k = PICK * h + 8 * S_TILES.index(t)
                            y = ys[k : k + 8]
                        if t in N_TILES:
                            k = PICK * h + 8 * N_TILES.index(t)
                            y = jnp.where(tab_ref[6, tr] > 0, y, yn[k : k + 8]) if t in S_TILES else yn[k : k + 8]
                        flow = flows[l, 0, tr] * x + flows[l, 1, tr] * y - tab_ref[4, tr] * c
                        out.append(c + shrink * flow)
                staged[rows, lane_tile(j * (TW // 128) + l)] = jnp.concatenate(out, axis=0).astype(BF16)

    def stores(j):
        at = pl.ds(j * TW, TW)
        return pltpu.make_async_copy(staged.at[:, at], out_hbm.at[:, at], sems.at[2 * parts + j])

    pair = H // TW
    wait_part(0)
    fill_part(0, "s")
    wait_part(1)
    fill_part(1, "sn")
    for g in range(2, parts):
        wait_part(g)
        fill_part(g, "n" if g == parts - 1 else "sn")
        lax.fori_loop((g - 2) * pair, (g - 1) * pair, lambda j, c: (output(j), c)[1], 0)
        for j in range((g - 2) * pair, (g - 1) * pair):
            stores(j).start()
    for j in range(points // TW):
        stores(j).wait()


def move(tab, winds, links, spectra, before, after, base, base_h):
    points = links.shape[1]
    extended = points + 2 * H
    return pl.pallas_call(
        move_kernel,
        in_specs=[HERE] * 3 + [AWAY] * 5,
        out_specs=[AWAY, HERE],
        out_shape=[jax.ShapeDtypeStruct((K, points), BF16), jax.ShapeDtypeStruct((8, 128), F32)],
        scratch_shapes=[
            pltpu.VMEM((K, extended), BF16),
            pltpu.VMEM((K, extended), F32),
            pltpu.VMEM((K, extended), BF16),
            pltpu.VMEM((18 * PICK, points + H), BF16),
            pltpu.VMEM((18 * PICK, points + H), BF16),
            pltpu.VMEM((K, points), BF16),
            pltpu.VMEM((18 * PICK, TW), F32),
            pltpu.VMEM((18 * PICK, TW), F32),
            pltpu.VMEM((TW // 128, 2, HALF, 128), F32),
            pltpu.SemaphoreType.DMA((2 * (points // H + 2) + points // TW,)),
        ],
        compiler_params=params(BIG),
        cost_estimate=cost(2 * 2 * 18 * PICK * (TW + H) * points, K * points * 8),
        name="move",
    )(tab, winds, links, spectra, before, after, base, base_h)


def cell_kernel(got_ref, push_ref, pusht_ref, air_ref, wait_ref, wind_ref, rough_ref, left, right):
    capacity, blocks = pusht_ref.shape
    lat_dev = air_ref.shape[1]
    values = got_ref[...].reshape(blocks, 4 * capacity).T
    high = values.astype(BF16).astype(F32)
    low = values - high
    for r in range(capacity):
        cols = slice(r * blocks, (r + 1) * blocks)
        at_row = iota((lat_dev, blocks), 0) == (pusht_ref[r : r + 1, :] >> 7)
        for part, source in enumerate((high, low)):
            rows = [
                jnp.where(at_row, source[c * capacity + r : c * capacity + r + 1, :], 0.0) for c in range(4)
            ]
            left[part * 4 * lat_dev : (part + 1) * 4 * lat_dev, cols] = jnp.concatenate(rows, axis=0).astype(BF16)
        right[cols, :] = hot(iota((blocks, 128), 1) == (push_ref[:, r : r + 1] & 127))
    sums = jnp.dot(left[...], right[...], preferred_element_type=F32)
    sums = sums[: 4 * lat_dev] + sums[4 * lat_dev :]
    sx, sy, rough, share = (sums[c * lat_dev : (c + 1) * lat_dev] for c in range(4))
    count = jnp.maximum(share, 1.0)
    wind_ref[0] = air_ref[0] - 0.5 * (sx / count)
    wind_ref[1] = air_ref[1] - 0.5 * (sy / count)
    rough_ref[...] = rough / count


def cells(got, push, pusht, air_state, wait):
    capacity, blocks = pusht.shape
    lat_dev = air_state.shape[1]
    return pl.pallas_call(
        cell_kernel,
        in_specs=[HERE] * 4 + [AWAY],
        out_specs=[HERE] * 2,
        out_shape=[
            jax.ShapeDtypeStruct(air_state.shape, F32),
            jax.ShapeDtypeStruct(air_state.shape[1:], F32),
        ],
        scratch_shapes=[
            pltpu.VMEM((8 * lat_dev, capacity * blocks), BF16),
            pltpu.VMEM((capacity * blocks, 128), BF16),
        ],
        compiler_params=params(BIG),
        cost_estimate=cost(2 * 8 * lat_dev * 128 * capacity * blocks, 400000),
        name="cells",
    )(got, push, pusht, air_state, wait)


def chain(axis, step):
    peers = lax.axis_size(axis)
    pairs = [(i, i + 1) for i in range(peers - 1)]
    return pairs if step > 0 else [(j, i) for i, j in pairs]


def shards(spectra, interact, sea_mask, sea_tile, push_list, neighbors, air_wind, diffusion):
    both = ("wave", "atm")
    tab = jnp.asarray(row_tables())
    lat_total = air_wind.shape[1] * lax.axis_size("atm")
    points = spectra.shape[1]
    tiles = points // TW
    push = push_list[0]
    mask = sea_mask.reshape(1, points)

    pack = jnp.concatenate([air_wind, diffusion[None]], axis=0)
    above = lax.ppermute(pack[:, -8:], "atm", chain("atm", 1))
    below = lax.ppermute(pack[:, :8], "atm", chain("atm", -1))
    mid = jnp.concatenate([above, pack, below], axis=1)
    left = lax.ppermute(mid, "wave", chain("wave", 1))
    right = lax.ppermute(mid, "wave", chain("wave", -1))

    pts, pusht, to_prev, to_next = prepare(sea_tile.reshape(1, points), mask, push, spectra)
    held, to_prev, to_next = lax.optimization_barrier((mid, to_prev, to_next))
    base = base_own(interact, spectra, mask, 0, tiles, held)
    before = lax.ppermute(to_next, both, chain(both, 1))
    after = lax.ppermute(to_prev, both, chain(both, -1))

    air_state, outgoing = air(lat_total, held, left, right, pusht, base)
    arrived = lax.all_to_all(outgoing, both, split_axis=0, concat_axis=0, tiled=True)
    base_h = base_halo(interact, before, after, outgoing)

    outbound, winds = stresses(tab, arrived, pts, spectra, before, after, base_h)
    inbound = lax.all_to_all(outbound, both, split_axis=0, concat_axis=0, tiled=True)
    wave_spectra, token = move(tab, winds, neighbors, spectra, before, after, base, base_h)
    surface_wind, roughness = cells(inbound, push, pusht, air_state, token)
    return (wave_spectra, surface_wind, roughness)


def solution(mesh):
    placed = (
        P(None, ("wave", "atm")),
        P(),
        P(("wave", "atm")),
        P(("wave", "atm")),
        P(("wave", "atm"), None, None),
        P(None, ("wave", "atm")),
        P(None, "atm", "wave"),
        P("atm", "wave"),
    )
    return jax.shard_map(
        shards,
        mesh=mesh,
        in_specs=placed,
        out_specs=(P(None, ("wave", "atm")), P(None, "atm", "wave"), P("atm", "wave")),
        check_vma=False,
    )
```

time: 140 us -> 100 us (0.71)
  local copies, waits for them, and re-layouts: 22.2 us -> 2.22 us
  blocking collectives: 19 us -> 0 us
  waiting for transfers between devices: 16.4 us -> 0.98 us
  starting transfers between devices: 28.7 us -> 39.1 us
  Pallas kernels: 51.8 us -> 55.6 us
    unnamed x31 -> x13, local copies, waits for them, and re-layouts: 22.2 us -> 2.22 us
    all_to_all x1 -> x0, blocking collectives: 19 us -> none  [shards(): lax.all_to_all(outbound, both, split_axis=0, concat_axis=0, tiled=True)]
    all_to_all x0 -> x1, starting transfers between devices: none -> 8.84 us  [shards(): lax.all_to_all(outbound, both, split_axis=0, concat_axis=0, tiled=True)]
    ppermute x1, waiting for transfers between devices: 7.69 us -> 0.01 us  [shards(): above = lax.ppermute(pack[:, -8:], 'atm', chain('atm', 1))]
    ppermute x1, waiting for transfers between devices: 4.4 us -> 0.01 us  [shards(): below = lax.ppermute(pack[:, :8], 'atm', chain('atm', -1))]
    ppermute x1, waiting for transfers between devices: 3.78 us -> 0.01 us  [shards(): right = lax.ppermute(mid, 'wave', chain('wave', -1))]
    pallas_call x1, Pallas kernels: 5.69 us -> 8.82 us  [base_halo(): pl.pallas_call(base_halo_kernel, grid=(2 * n,), in_specs=[pl.BlockSpec((K...]
  transfers between devices with their start and end apart: 7 -> 8, of which waited for: 4 -> 1; matrix products, arithmetic and copies ran while one was open for 0% -> 1% of each run, Pallas kernels for 18% -> 48%
where the time goes in v1:
time: 100 us; the launch traced here: 99.5 us
  Pallas kernels  55.6 us (56%)
  starting transfers between devices  39.1 us (39%)
  local copies, waits for them, and re-layouts  2.22 us (2%)
    pallas_call x1, Pallas kernels, move(): pl.pallas_call(move_kernel, in_specs=[HERE] * 3 + [AWAY] * 5, out_specs=[...  19.6 us
    pallas_call x1, Pallas kernels, base_own(): pl.pallas_call(base_kernel, grid=(count,), in_specs=[pl.BlockSpec((K, K),...  14.5 us
    all_to_all x1, starting transfers between devices, shards(): lax.all_to_all(outgoing, both, split_axis=0, concat_axis=0, tiled=True)  12.6 us
    all_to_all x1, starting transfers between devices, shards(): lax.all_to_all(outbound, both, split_axis=0, concat_axis=0, tiled=True)  8.84 us
    pallas_call x1, Pallas kernels, base_halo(): pl.pallas_call(base_halo_kernel, grid=(2 * n,), in_specs=[pl.BlockSpec((K...  8.82 us
    pallas_call x1, Pallas kernels, stresses(): pl.pallas_call(stress_kernel, in_specs=[HERE] * 3 + [AWAY] * 4, out_specs...  5.2 us
    ppermute x1, starting transfers between devices, shards(): above = lax.ppermute(pack[:, -8:], 'atm', chain('atm', 1))  4.92 us
    ppermute x1, starting transfers between devices, shards(): left = lax.ppermute(mid, 'wave', chain('wave', 1))  3.99 us
  transfers between devices with their start and end apart: 8, of which 1 were waited for; matrix products, arithmetic and copies ran while one was open for 1% of the time, Pallas kernels for 48%

profile of v1, /device:TPU:1, one launch (start us, length us, event | category | flops | bytes accessed | tf_op | source)
XLA Modules:
  0.0 99.5 jit_solution(5050777070110956698)
XLA Ops:
  0.7 0.8 pad_maximum_fusion.2
  1.4 4.9 %collective-permute-start = (f32[3,8,128]{2,1,0:T(8,128)S(1)}, f32[3,8,128]{2,1,0:T(8,128)S(1)}, u32[]{:S(2)}, u32[]{:S(2)}) collective-permute-start(f32[3,8,128]{2,1,0:T(8,128)S(1)} %get-tuple-element.33), channel_id=1, source_target_pairs={{0,1},{1,2},{2,3},{3,4},{4,5},{5,6},{6,7},{8,9},{9,10},{10,11},{11... | collective-permute-start | bytes 36872 | tf_op jit(solution)/shard_map/ppermute | solution.py:641
  6.4 1.9 %collective-permute-start.1 = (f32[3,8,128]{2,1,0:T(8,128)S(1)}, f32[3,8,128]{2,1,0:T(8,128)S(1)}, u32[]{:S(2)}, u32[]{:S(2)}) collective-permute-start(f32[3,8,128]{2,1,0:T(8,128)S(1)} %get-tuple-element.34), channel_id=1, source_target_pairs={{1,0},{2,1},{3,2},{4,3},{5,4},{6,5},{7,6},{9,8},{10,9},{11,10},{12... | collective-permute-start | bytes 36872 | tf_op jit(solution)/shard_map/ppermute | solution.py:642
  8.3 0.8 copy.12
  9.1 0.0 copy-start.2
  9.1 0.7 copy-done.2
  9.8 0.7 copy-done.3
  10.5 2.8 %prepare.1 = (f32[8,2048]{1,0:T(8,128)S(1)}, s32[32,128]{1,0:T(8,128)S(1)}, bf16[1312,512]{1,0:T(8,128)(2,1)S(1)}, bf16[1312,512]{1,0:T(8,128)(2,1)}) custom-call(s32[1,2048]{1,0:T(1,128)S(1)} %bitcast.6, s32[1,2048]{1,0:T(1,128)S(1)} %bitcast.7, s32[128,32]{1,0:T(8,128)S(1)} %bitcast.4, bf16[1296,2048]{1,0:T(8,128)(2,1)} %s_hbm.3), custom_call_target="tpu_custom_call" | custom-call | flops 268435456 | bytes 5373952 | tf_op jit(solution)/shard_map/prepare/pallas_call | solution.py:126
  13.3 0.0 collective-permute-done
  13.4 3.6 %collective-permute-start.4 = (bf16[1312,512]{1,0:T(8,128)(2,1)}, bf16[1312,512]{1,0:T(8,128)(2,1)S(1)}, u32[]{:S(2)}, u32[]{:S(2)}) collective-permute-start(bf16[1312,512]{1,0:T(8,128)(2,1)} %get-tuple-element.24), channel_id=1, source_target_pairs={{0,1},{1,2},{2,3},{3,4},{4,5},{5,6},{6,7},{7,8},{8,9},{9,10},{10,1... | collective-permute-start | bytes 4030472 | tf_op jit(solution)/shard_map/ppermute | solution.py:650
  17.1 1.9 %collective-permute-start.5 = (bf16[1312,512]{1,0:T(8,128)(2,1)S(1)}, bf16[1312,512]{1,0:T(8,128)(2,1)}, u32[]{:S(2)}, u32[]{:S(2)}) collective-permute-start(bf16[1312,512]{1,0:T(8,128)(2,1)S(1)} %get-tuple-element.25), channel_id=1, source_target_pairs={{1,0},{2,1},{3,2},{4,3},{5,4},{6,5},{7,6},{8,7},{9,8},{10,9},{11,1... | collective-permute-start | bytes 4030472 | tf_op jit(solution)/shard_map/ppermute | solution.py:651
  19.0 1.3 %collective-permute-start.3 = (f32[3,80,128]{2,1,0:T(8,128)S(1)}, f32[3,80,128]{2,1,0:T(8,128)S(1)}, u32[]{:S(2)}, u32[]{:S(2)}) collective-permute-start(f32[3,80,128]{2,1,0:T(8,128)S(1)} %pad_maximum_fusion.wait_ref.a), channel_id=1, source_target_pairs={{8,0},{16,8},{24,16},{32,24},{40,32},{48,40},{56,48},{64,56},{72,6... | collective-permute-start | bytes 368648 | tf_op jit(solution)/shard_map/ppermute | solution.py:645
  20.3 4.0 %collective-permute-start.2 = (f32[3,80,128]{2,1,0:T(8,128)S(1)}, f32[3,80,128]{2,1,0:T(8,128)S(1)}, u32[]{:S(2)}, u32[]{:S(2)}) collective-permute-start(f32[3,80,128]{2,1,0:T(8,128)S(1)} %pad_maximum_fusion.wait_ref.a), channel_id=1, source_target_pairs={{0,8},{8,16},{16,24},{24,32},{32,40},{40,48},{48,56},{56,64},{64,7... | collective-permute-start | bytes 368648 | tf_op jit(solution)/shard_map/ppermute | solution.py:644
  24.3 14.5 %base_own.1.wait.b_hbm = f32[1296,2048]{1,0:T(8,128)} custom-call(bf16[1296,1296]{1,0:T(8,128)(2,1)} %it_ref.3, bf16[1296,2048]{1,0:T(8,128)(2,1)} %s_hbm.3, s32[1,2048]{1,0:T(1,128)S(1)} %bitcast.8, f32[3,80,128]{2,1,0:T(8,128)S(1)} %pad_maximum_fusion.wait_ref.a), custom_call_target="tpu_custom_call" | custom-call | flops 6879707136 | bytes 3359232 | tf_op jit(solution)/shard_map/base_own/pallas_call | solution.py:184
  38.8 2.2 %air.1 = (f32[2,64,128]{2,1,0:T(8,128)S(1)}, f32[128,1,256]{2,1,0:T(1,128)}) custom-call(f32[3,80,128]{2,1,0:T(8,128)S(1)} %pad_maximum_fusion.wait_ref.a, f32[3,80,128]{2,1,0:T(8,128)S(1)} %collective-permute-done.2.b, f32[3,80,128]{2,1,0:T(8,128)S(1)} %collective-permute-done.3.c, s32[32,128]{1,0:T(8,128)S(1)} %get-tuple-element.21.d.pusht_ref, ...), custom_call_target="tpu_custom_call" | custom-call | flops 134217728 | bytes 600000 | tf_op jit(solution)/shard_map/air/pallas_call | solution.py:286
  40.9 12.6 %all-to-all-start = ((f32[128,1,256]{2,1,0:T(1,128)}), f32[128,1,256]{2,1,0:T(1,128)S(1)}, u32[]{:S(2)}, u32[]{:S(2)}) async-start(f32[128,1,256]{2,1,0:T(1,128)} %get-tuple-element.22.wait_ref), calls=%async_computation | async-start | bytes 262144 | tf_op jit(solution)/shard_map/all_to_all | solution.py:654
  53.6 0.0 copy-start
  53.6 0.0 collective-permute-done.5.sa_ref.pa_ref.sa_hbm
  53.6 8.8 %base_halo.1.wait_ref.bh_hbm = f32[1296,1024]{1,0:T(8,128)} custom-call(bf16[1296,1296]{1,0:T(8,128)(2,1)} %it_ref.3, bf16[1312,512]{1,0:T(8,128)(2,1)S(1)} %collective-permute-done.4.sb_ref.pb_ref.sb_hbm, bf16[1312,512]{1,0:T(8,128)(2,1)} %collective-permute-done.5.sa_ref.pa_ref.sa_hbm, bf16[1312,512]{1,0:T(8,128)(2,1)S(1)} %collective-permute-done.4.sb_ref.pb_ref.sb_hbm, ...), custom_call_target="tpu_custom_call" | custom-call | flops 3439853568 | bytes 3359232 | tf_op jit(solution)/shard_map/base_halo/pallas_call | solution.py:218
  62.4 1.0 all-to-all-done.got_ref
  63.4 5.2 %stress.1 = (f32[128,1,128]{2,1,0:T(1,128)}, f32[8,3072]{1,0:T(8,128)S(1)}) custom-call(f32[7,72,128]{2,1,0:T(8,128)S(1)} %copy-done, f32[128,1,256]{2,1,0:T(1,128)S(1)} %all-to-all-done.got_ref, f32[8,2048]{1,0:T(8,128)S(1)} %get-tuple-element.23.p_ref, bf16[1296,2048]{1,0:T(8,128)(2,1)} %s_hbm.3, ...), custom_call_target="tpu_custom_call" | custom-call | flops 26542080 | bytes 5308416 | tf_op jit(solution)/shard_map/stress/pallas_call | solution.py:407
  68.6 8.8 %all-to-all-start.1 = ((f32[128,1,128]{2,1,0:T(1,128)}), f32[128,1,128]{2,1,0:T(1,128)S(1)}, u32[]{:S(2)}, u32[]{:S(2)}) async-start(f32[128,1,128]{2,1,0:T(1,128)} %get-tuple-element.28), calls=%async_computation.1 | async-start | bytes 131072 | tf_op jit(solution)/shard_map/all_to_all | solution.py:658
  77.5 19.6 %move.1 = (bf16[1296,2048]{1,0:T(8,128)(2,1)}, f32[8,128]{1,0:T(8,128)S(1)}) custom-call(f32[7,72,128]{2,1,0:T(8,128)S(1)} %copy-done, f32[8,3072]{1,0:T(8,128)S(1)} %get-tuple-element.26.winds_ref, s32[4,2048]{1,0:T(4,128)S(1)} %copy-done.1, bf16[1296,2048]{1,0:T(8,128)(2,1)} %s_hbm.3, bf16[1312,512]{1,0:T(8,128)(2,1)S(1)} %collective-permute-done.4.sb_ref.pb_ref.sb_hbm, ...), custom_call_target="tpu_custom_call" | custom-call | flops 5435817984 | bytes 21233664 | tf_op jit(solution)/shard_map/move/pallas_call | solution.py:557
  97.1 2.5 %cells.1 = (f32[2,64,128]{2,1,0:T(8,128)}, f32[64,128]{1,0:T(8,128)}) custom-call(f32[128,1,128]{2,1,0:T(1,128)S(1)} %all-to-all-done.1.got_ref, s32[128,32]{1,0:T(8,128)S(1)} %bitcast.5, s32[32,128]{1,0:T(8,128)S(1)} %get-tuple-element.21.d.pusht_ref, f32[2,64,128]{2,1,0:T(8,128)S(1)} %get-tuple-element.29.air_ref, f32[8,128]{1,0:T(8,128)S(1)} %get-tuple-element.30.wait_ref), custom_call_target="tpu_custom_call" | custom-call | flops 536870912 | bytes 400000 | tf_op jit(solution)/shard_map/cells/pallas_call | solution.py:607
  (14 shorter events, 0.0 us)
Async XLA Ops:
  0.6 12.7 %copy-start.4 = (f32[2,64,128]{2,1,0:T(8,128)S(1)}, f32[2,64,128]{2,1,0:T(8,128)}, u32[]{:S(2)}) copy-start(f32[2,64,128]{2,1,0:T(8,128)} %param.15) | copy-start | bytes 196612
  0.6 12.7 %copy-start.5 = (f32[64,128]{1,0:T(8,128)S(1)}, f32[64,128]{1,0:T(8,128)}, u32[]{:S(2)}) copy-start(f32[64,128]{1,0:T(8,128)} %param.16) | copy-start | bytes 98308
  1.4 11.9 %collective-permute-start = (f32[3,8,128]{2,1,0:T(8,128)S(1)}, f32[3,8,128]{2,1,0:T(8,128)S(1)}, u32[]{:S(2)}, u32[]{:S(2)}) collective-permute-start(f32[3,8,128]{2,1,0:T(8,128)S(1)} %get-tuple-element.33), channel_id=1, source_target_pairs={{0,1},{1,2},{2,3},{3,4},{4,5},{5,6},{6,7},{8,9},{9,10},{10,11},{11... | collective-permute-start | bytes 36872 | tf_op jit(solution)/shard_map/ppermute | solution.py:641
  6.4 7.0 %collective-permute-start.1 = (f32[3,8,128]{2,1,0:T(8,128)S(1)}, f32[3,8,128]{2,1,0:T(8,128)S(1)}, u32[]{:S(2)}, u32[]{:S(2)}) collective-permute-start(f32[3,8,128]{2,1,0:T(8,128)S(1)} %get-tuple-element.34), channel_id=1, source_target_pairs={{1,0},{2,1},{3,2},{4,3},{5,4},{6,5},{7,6},{9,8},{10,9},{11,10},{12... | collective-permute-start | bytes 36872 | tf_op jit(solution)/shard_map/ppermute | solution.py:642
  9.1 0.7 copy-start.2
  9.8 0.7 copy-start.3
  13.4 40.2 %collective-permute-start.4 = (bf16[1312,512]{1,0:T(8,128)(2,1)}, bf16[1312,512]{1,0:T(8,128)(2,1)S(1)}, u32[]{:S(2)}, u32[]{:S(2)}) collective-permute-start(bf16[1312,512]{1,0:T(8,128)(2,1)} %get-tuple-element.24), channel_id=1, source_target_pairs={{0,1},{1,2},{2,3},{3,4},{4,5},{5,6},{6,7},{7,8},{8,9},{9,10},{10,1... | collective-permute-start | bytes 4030472 | tf_op jit(solution)/shard_map/ppermute | solution.py:650
  17.1 36.5 %collective-permute-start.5 = (bf16[1312,512]{1,0:T(8,128)(2,1)S(1)}, bf16[1312,512]{1,0:T(8,128)(2,1)}, u32[]{:S(2)}, u32[]{:S(2)}) collective-permute-start(bf16[1312,512]{1,0:T(8,128)(2,1)S(1)} %get-tuple-element.25), channel_id=1, source_target_pairs={{1,0},{2,1},{3,2},{4,3},{5,4},{6,5},{7,6},{8,7},{9,8},{10,9},{11,1... | collective-permute-start | bytes 4030472 | tf_op jit(solution)/shard_map/ppermute | solution.py:651
  19.0 19.8 %collective-permute-start.3 = (f32[3,80,128]{2,1,0:T(8,128)S(1)}, f32[3,80,128]{2,1,0:T(8,128)S(1)}, u32[]{:S(2)}, u32[]{:S(2)}) collective-permute-start(f32[3,80,128]{2,1,0:T(8,128)S(1)} %pad_maximum_fusion.wait_ref.a), channel_id=1, source_target_pairs={{8,0},{16,8},{24,16},{32,24},{40,32},{48,40},{56,48},{64,56},{72,6... | collective-permute-start | bytes 368648 | tf_op jit(solution)/shard_map/ppermute | solution.py:645
  20.3 18.5 %collective-permute-start.2 = (f32[3,80,128]{2,1,0:T(8,128)S(1)}, f32[3,80,128]{2,1,0:T(8,128)S(1)}, u32[]{:S(2)}, u32[]{:S(2)}) collective-permute-start(f32[3,80,128]{2,1,0:T(8,128)S(1)} %pad_maximum_fusion.wait_ref.a), channel_id=1, source_target_pairs={{0,8},{8,16},{16,24},{24,32},{32,40},{40,48},{48,56},{56,64},{64,7... | collective-permute-start | bytes 368648 | tf_op jit(solution)/shard_map/ppermute | solution.py:644
  40.9 22.4 %all-to-all-start = ((f32[128,1,256]{2,1,0:T(1,128)}), f32[128,1,256]{2,1,0:T(1,128)S(1)}, u32[]{:S(2)}, u32[]{:S(2)}) async-start(f32[128,1,256]{2,1,0:T(1,128)} %get-tuple-element.22.wait_ref), calls=%async_computation | async-start | bytes 262144 | tf_op jit(solution)/shard_map/all_to_all | solution.py:654
  53.6 9.8 %copy-start = (f32[7,72,128]{2,1,0:T(8,128)S(1)}, f32[7,72,128]{2,1,0:T(8,128)}, u32[]{:S(2)}) copy-start(f32[7,72,128]{2,1,0:T(8,128)} %constant.2.clone.tab_ref) | copy-start | bytes 774148
  63.4 14.1 %copy-start.1 = (s32[4,2048]{1,0:T(4,128)S(1)}, s32[4,2048]{1,0:T(4,128)}, u32[]{:S(2)}) copy-start(s32[4,2048]{1,0:T(4,128)} %link_ref.1) | copy-start | bytes 98308
  68.6 28.5 %all-to-all-start.1 = ((f32[128,1,128]{2,1,0:T(1,128)}), f32[128,1,128]{2,1,0:T(1,128)S(1)}, u32[]{:S(2)}, u32[]{:S(2)}) async-start(f32[128,1,128]{2,1,0:T(1,128)} %get-tuple-element.28), calls=%async_computation.1 | async-start | bytes 131072 | tf_op jit(solution)/shard_map/all_to_all | solution.py:658

commit v2 on v1

v2 whole, which is shorter than its diff:
```python
import math

import jax
import jax.numpy as jnp
import numpy as np
from jax import lax
from jax.experimental import pallas as pl
from jax.experimental.pallas import tpu as pltpu
from jax.sharding import PartitionSpec as P

ND = 36
NF = 36
K = ND * NF
H = 512
ATM_STEPS = 4
TW = 256
CH = 144
NCH = K // CH
HALF = 72
HALO_ROWS = K + 16
F32 = jnp.float32
BF16 = jnp.bfloat16
I32 = jnp.int32

S_TILES = (0, 1, 2, 4, 5, 6)
N_TILES = (2, 3, 4, 6, 7, 8)
PICK = 8 * len(S_TILES)


def row_tables():
    r = np.arange(HALF)
    d = r % ND
    angle = (d + 0.5) * (2.0 * math.pi / ND)
    up = np.power(1.1, r // ND)
    cosine, sine = np.cos(angle), np.sin(angle)
    reach = 0.7 / up
    rows = [
        up * cosine,
        up * sine,
        np.abs(reach * cosine),
        np.abs(reach * sine),
        np.abs(reach * cosine) + np.abs(reach * sine),
        (cosine > 0).astype(np.float64),
        (sine > 0).astype(np.float64),
    ]
    table = np.stack(rows).astype(np.float32)
    return np.ascontiguousarray(np.broadcast_to(table[:, :, None], table.shape + (128,)))


COS_POS = [bool(math.cos((d + 0.5) * 2.0 * math.pi / ND) > 0) for d in range(ND)]


def west_kind(tile):
    signs = {COS_POS[(8 * tile + s) % ND] for s in range(8)}
    return "both" if len(signs) == 2 else ("west" if True in signs else "east")


def iota(shape, dim):
    return lax.broadcasted_iota(I32, shape, dim)


def hot(mask):
    return jnp.where(mask, 1.0, 0.0).astype(BF16)


def contract(a, b, da, db):
    return lax.dot_general(a, b, (((da,), (db,)), ((), ())), preferred_element_type=F32)


def params(megabytes):
    return pltpu.CompilerParams(vmem_limit_bytes=megabytes << 20)


BIG = 52


HERE = pl.BlockSpec(memory_space=pltpu.VMEM)
AWAY = pl.BlockSpec(memory_space=pl.ANY)


def cost(flops, data):
    return pl.CostEstimate(flops=flops, bytes_accessed=data, transcendentals=0)


def prepare_kernel(code_ref, push_ref, s_ref, pts_ref, pusht_ref, to_prev, to_next, rims, sems):
    blocks = push_ref.shape[0]
    points = code_ref.shape[1]
    ends = ((to_prev, 0), (to_next, points - H))
    loads = [
        pltpu.make_async_copy(s_ref.at[:, pl.ds(lo, H)], rims.at[k, pl.ds(0, K), :], sems.at[k])
        for k, (out, lo) in enumerate(ends)
    ]
    for load in loads:
        load.start()
    pusht_ref[...] = push_ref[...].astype(F32).T.astype(I32)
    before = hot(iota((TW, TW), 0) < iota((TW, TW), 1))
    ones = jnp.ones((TW, TW), BF16)
    running = jnp.zeros((blocks, TW), F32)
    for c in range(points // TW):
        cols = slice(c * TW, (c + 1) * TW)
        tile = code_ref[0:1, cols]
        same = iota((blocks, TW), 0) == tile
        onehot = hot(same)
        earlier = contract(onehot, before, 1, 0) + running
        rank = jnp.sum(jnp.where(same, earlier, 0.0), axis=0, keepdims=True)
        running = running + contract(onehot, ones, 1, 0)
        pts_ref[0:1, cols] = tile.astype(F32)
        pts_ref[1:2, cols] = rank
        pts_ref[2:3, cols] = code_ref[1:2, cols].astype(F32)
        pts_ref[3:8, cols] = jnp.zeros((5, TW), F32)
    stores = []
    for k, (out, lo) in enumerate(ends):
        rows = jnp.concatenate([pts_ref[:, lo : lo + H], jnp.zeros((8, H), F32)], axis=0)
        rims[k, K:, :] = rows.astype(BF16)
        loads[k].wait()
        store = pltpu.make_async_copy(rims.at[k], out, sems.at[2 + k])
        store.start()
        stores.append(store)
    for store in stores:
        store.wait()


def prepare(code, push, spectra):
    blocks, capacity = push.shape
    points = code.shape[1]
    return pl.pallas_call(
        prepare_kernel,
        in_specs=[HERE, HERE, AWAY],
        out_specs=[HERE, HERE, AWAY, AWAY],
        out_shape=[
            jax.ShapeDtypeStruct((8, points), F32),
            jax.ShapeDtypeStruct((capacity, blocks), I32),
            jax.ShapeDtypeStruct((HALO_ROWS, H), BF16),
            jax.ShapeDtypeStruct((HALO_ROWS, H), BF16),
        ],
        scratch_shapes=[pltpu.VMEM((2, HALO_ROWS, H), BF16), pltpu.SemaphoreType.DMA((4,))],
        compiler_params=params(BIG),
        cost_estimate=cost(2 * 2 * blocks * TW * points, 4 * HALO_ROWS * H * 2),
        name="prepare",
    )(code, push, spectra)


CUTS = (0, CH, 3 * CH, 6 * CH, K)


def columns(i):
    return pl.ds(pl.multiple_of(i * TW, TW), TW)


def interact_kernel(it_hbm, *refs):
    *sources, wait_ref, out_hbm, mean_ref, it_ref, s_ref, out_ref, sems = refs
    tiles = out_hbm.shape[1] // TW
    each = tiles // len(sources)
    parts = len(CUTS) - 1
    loads = [
        pltpu.make_async_copy(
            sources[i // each].at[pl.ds(0, K), pl.ds(i % each * TW, TW)], s_ref.at[i], sems.at[i]
        )
        for i in range(tiles)
    ]
    pieces = [
        pltpu.make_async_copy(it_hbm.at[pl.ds(a, b - a), :], it_ref.at[pl.ds(a, b - a), :], sems.at[tiles + c])
        for c, (a, b) in enumerate(zip(CUTS[:-1], CUTS[1:]))
    ]

    def store(i):
        return pltpu.make_async_copy(out_ref.at[i], out_hbm.at[:, columns(i)], sems.at[tiles + parts + i])

    def mean_of(i):
        acc = jnp.zeros((HALF, TW), F32)
        for m in range(NCH):
            s = s_ref[i, m * CH : (m + 1) * CH, :].astype(F32)
            acc = acc + (s[:HALF] + s[HALF:])
        mean = jnp.sum(acc, axis=0, keepdims=True) * (1.0 / K)
        mean_ref[:, columns(i)] = jnp.broadcast_to(mean, (mean_ref.shape[0], TW))

    pieces[0].start()
    loads[0].start()
    pieces[1].start()
    loads[0].wait()
    pieces[2].start()
    loads[1].start()
    mean_of(0)
    for c, (a, b) in enumerate(zip(CUTS[:-1], CUTS[1:])):
        pieces[c].wait()
        if c == 0:
            pieces[3].start()
        out_ref[0, a:b, :] = jnp.dot(it_ref[a:b, :], s_ref[0], preferred_element_type=F32).astype(BF16)
    store(0).start()
    for load in loads[2:]:
        load.start()

    def body(i, carry):
        pltpu.make_async_copy(sources[0].at[pl.ds(0, K), pl.ds(0, TW)], s_ref.at[i], sems.at[i]).wait()
        out_ref[i] = jnp.dot(it_ref[...], s_ref[i], preferred_element_type=F32).astype(BF16)
        store(i).start()
        mean_of(i)
        return carry

    lax.fori_loop(1, tiles, body, 0)
    for i in range(tiles):
        store(i).wait()


def interactions(interact, sources, points, wait, name):
    tiles = points // TW
    return pl.pallas_call(
        interact_kernel,
        in_specs=[AWAY] * (len(sources) + 2),
        out_specs=[AWAY, HERE],
        out_shape=[jax.ShapeDtypeStruct((K, points), BF16), jax.ShapeDtypeStruct((8, points), F32)],
        scratch_shapes=[
            pltpu.VMEM((K, K), BF16),
            pltpu.VMEM((tiles, K, TW), BF16),
            pltpu.VMEM((tiles, K, TW), BF16),
            pltpu.SemaphoreType.DMA((2 * tiles + len(CUTS) - 1,)),
        ],
        compiler_params=params(BIG),
        cost_estimate=cost(2 * K * K * points, K * points * 4),
        name=name,
    )(interact, *sources, wait)


def air_kernel(lat_total, mid_ref, left_ref, right_ref, pusht_ref, air_ref, out_ref, slots):
    rows = mid_ref.shape[1]
    lat_dev = rows - 16
    lane = iota((rows, 128), 1)

    def field(i):
        side = jnp.where(lane < 8, right_ref[i], jnp.where(lane >= 120, left_ref[i], 0.0))
        return jnp.concatenate([mid_ref[i], side], axis=1)

    east, north, spread = field(0), field(1), field(2)
    first = lax.axis_index("atm") * lat_dev - 8
    row = (iota((rows, 256), 0) + first).astype(F32)
    turning = 0.05 + 0.1 * row / lat_total

    def laplace(w):
        around = pltpu.roll(w, rows - 1, 0) + pltpu.roll(w, 1, 0) + pltpu.roll(w, 255, 1) + pltpu.roll(w, 1, 1)
        return around - 4.0 * w

    for _ in range(ATM_STEPS):
        e = east + spread * laplace(east) + turning * north
        n = north + spread * laplace(north) - turning * east
        east, north = e, n
    east = east[8 : 8 + lat_dev, :128]
    north = north[8 : 8 + lat_dev, :128]
    air_ref[0] = east
    air_ref[1] = north
    field_t = jnp.concatenate([east.T, north.T], axis=0).astype(BF16)
    capacity, blocks = pusht_ref.shape
    group = 4
    for g in range(capacity // group):
        cells = jnp.concatenate([pusht_ref[g * group + k : g * group + k + 1, :] for k in range(group)], axis=1)
        at_row = hot(iota((lat_dev, group * blocks), 0) == (cells >> 7))
        picked = jnp.dot(field_t, at_row, preferred_element_type=F32)
        at_col = iota((128, group * blocks), 0) == (cells & 127)
        for c in range(2):
            value = jnp.sum(jnp.where(at_col, picked[c * 128 : (c + 1) * 128], 0.0), axis=0, keepdims=True)
            for k in range(group):
                at = c * capacity + g * group + k
                slots[at : at + 1, :] = value[:, k * blocks : (k + 1) * blocks]
    own = slots[...]
    stacked = jnp.concatenate([pltpu.roll(own, 1, 1), own, pltpu.roll(own, blocks - 1, 1), jnp.zeros_like(own)], axis=0)
    out_ref[...] = stacked.T.reshape(out_ref.shape)


def air(lat_total, mid, left, right, pusht):
    capacity, blocks = pusht.shape
    lat_dev = mid.shape[1] - 16
    assert mid.shape[2] == 128 and blocks == 128
    return pl.pallas_call(
        lambda *refs: air_kernel(lat_total, *refs),
        in_specs=[HERE] * 4,
        out_specs=[HERE] * 2,
        out_shape=[
            jax.ShapeDtypeStruct((2, lat_dev, 128), F32),
            jax.ShapeDtypeStruct((blocks, 1, 8 * capacity), F32),
        ],
        scratch_shapes=[pltpu.VMEM((2 * capacity, blocks), F32)],
        compiler_params=params(BIG),
        cost_estimate=cost(2 * 256 * lat_dev * capacity * blocks, 600000),
        name="air",
    )(mid, left, right, pusht)


def winds_at(table, tile, rank):
    slots = table.shape[0] // 2
    tiles = table.shape[1]
    points = tile.shape[1]
    onehot = hot(iota((tiles, points), 0) == tile.astype(I32))
    values = jnp.dot(table, onehot, preferred_element_type=F32)
    at = iota((slots, points), 0) == rank.astype(I32)
    east = jnp.sum(jnp.where(at, values[:slots], 0.0), axis=0, keepdims=True)
    north = jnp.sum(jnp.where(at, values[slots:], 0.0), axis=0, keepdims=True)
    return east, north, onehot, at


def growth_pattern(tab_ref, east, north):
    return tab_ref[0] * (0.2 * east) + tab_ref[1] * (0.2 * north)


def step_scale(m, h):
    return 1.1 ** (4 * m + 2 * h - NF / 2)


SW = 512


def lane_tile(i):
    return pl.ds(pl.multiple_of(i * 128, 128), 128)


def stress_kernel(
    tab_ref, got_ref, p_ref, s_hbm, wait_ref, send_ref, winds_ref, s_ref, table, waves, sems
):
    points = p_ref.shape[1]
    blocks = got_ref.shape[0]
    slots = got_ref.shape[2] // 4
    groups = points // SW
    loads = [
        pltpu.make_async_copy(s_hbm.at[:, pl.ds(g * SW, SW)], s_ref.at[:, pl.ds(g * SW, SW)], sems.at[g])
        for g in range(groups)
    ]
    for load in loads[:2]:
        load.start()
    table[...] = got_ref[...].reshape(blocks, got_ref.shape[2]).T.astype(BF16)
    winds_ref[3:8, :] = jnp.zeros((5, winds_ref.shape[1]), F32)

    for g in range(groups):
        cols = slice(g * SW, (g + 1) * SW)
        east, north, _, _ = winds_at(table[slots : 2 * slots, :], p_ref[0:1, cols], p_ref[1:2, cols])
        mask = p_ref[2:3, cols]
        winds_ref[0:1, cols] = east * mask
        winds_ref[1:2, cols] = north * mask
        winds_ref[2:3, cols] = mask

    def tile(i, carry):
        at = lane_tile(i)
        pattern = growth_pattern(tab_ref, winds_ref[0:1, at], winds_ref[1:2, at])
        acc = jnp.zeros((HALF, 128), F32)
        for m in range(NCH):
            s = s_ref[m * CH : (m + 1) * CH, lane_tile(i)].astype(F32)
            for h in range(2):
                scale = step_scale(m, h)
                bent = jnp.maximum((scale * scale) * pattern - 0.25 * scale, 0.0)
                acc = acc + bent * s[h * HALF : (h + 1) * HALF]
        waves[0:1, lane_tile(i)] = jnp.sum(acc * tab_ref[0], axis=0, keepdims=True)
        waves[1:2, lane_tile(i)] = jnp.sum(acc * tab_ref[1], axis=0, keepdims=True)
        return carry

    per = SW // 128
    for g in range(groups):
        loads[g].wait()
        if g + 2 < groups:
            loads[g + 2].start()
        lax.fori_loop(g * per, (g + 1) * per, tile, 0)

    total = jnp.zeros((blocks, 2 * slots), F32)
    for g in range(groups):
        cols = slice(g * SW, (g + 1) * SW)
        east, north, mask = (winds_ref[k : k + 1, cols] for k in range(3))
        speed = jnp.sqrt(east * east + north * north + 0.25)
        stress_x = 0.3 * speed * east + mask * (waves[0:1, cols] * (0.4 / K))
        stress_y = 0.3 * speed * north + mask * (waves[1:2, cols] * (0.4 / K))
        rough = mask * 0.2 * jnp.sqrt(stress_x * stress_x + stress_y * stress_y + 0.01)
        onehot = hot(iota((blocks, SW), 0) == p_ref[0:1, cols].astype(I32))
        at = iota((slots // 2, SW), 0) == p_ref[1:2, cols].astype(I32)
        values = jnp.concatenate([jnp.where(at, v, 0.0) for v in (stress_x, stress_y, rough, mask)], axis=0)
        high = values.astype(BF16)
        rest = values - high.astype(F32)
        middle = rest.astype(BF16)
        low = (rest - middle.astype(F32)).astype(BF16)
        total = total + contract(
            jnp.concatenate([onehot] * 3, axis=1), jnp.concatenate([high, middle, low], axis=1), 1, 1
        )
    send_ref[...] = total.reshape(send_ref.shape)


def stresses(tab, got, pts, spectra, wait):
    points = spectra.shape[1]
    blocks = got.shape[0]
    capacity = got.shape[2] // 8
    return pl.pallas_call(
        stress_kernel,
        in_specs=[HERE] * 3 + [AWAY] * 2,
        out_specs=[HERE] * 2,
        out_shape=[
            jax.ShapeDtypeStruct((blocks, 1, 4 * capacity), F32),
            jax.ShapeDtypeStruct((8, points), F32),
        ],
        scratch_shapes=[
            pltpu.VMEM((K, points), BF16),
            pltpu.VMEM((8 * capacity, blocks), BF16),
            pltpu.VMEM((8, points), F32),
            pltpu.SemaphoreType.DMA((points // SW,)),
        ],
        compiler_params=params(BIG),
        cost_estimate=cost(10 * K * points, K * points * 2),
        name="stress",
    )(tab, got, pts, spectra, wait)


def chosen_rows(x, tiles):
    rows = [x[HALF * h + 8 * t : HALF * h + 8 * t + 8] for h in range(2) for t in tiles]
    return jnp.concatenate(rows, axis=0).astype(BF16)


def move_kernel(
    tab_ref, winds_ref, link_ref, got_ref, mean_ref, it_hbm, s_hbm, sb_hbm, sa_hbm, n_hbm,
    out_hbm, token, table, rim, rim_winds, it_ref, s_ref, n_ref, product, natural, south, north, staged, hots, south_y, north_y, flows, sems,
):
    points = link_ref.shape[1]
    parts = points // H + 2
    loads = []
    for g in range(parts):
        to = pl.ds(g * H, H)
        if g == 0:
            source = sb_hbm.at[pl.ds(0, K), :]
        elif g == parts - 1:
            source = sa_hbm.at[pl.ds(0, K), :]
        else:
            source = s_hbm.at[:, pl.ds((g - 1) * H, H)]
        loads.append(pltpu.make_async_copy(source, s_ref.at[:, to], sems.at[g]))
    matrix = pltpu.make_async_copy(it_hbm, it_ref, sems.at[parts])
    products = [
        pltpu.make_async_copy(n_hbm.at[:, pl.ds(g * H, H)], n_ref.at[:, pl.ds(g * H, H)], sems.at[parts + 3 + g])
        for g in range(parts - 2)
    ]
    places = [
        pltpu.make_async_copy(ref.at[pl.ds(K, 16), :], rim.at[k], sems.at[parts + 1 + k])
        for k, ref in enumerate((sb_hbm, sa_hbm))
    ]
    for place in places:
        place.start()

    order = (1, 0, *range(2, parts))

    def start_part(k):
        if k < parts:
            loads[order[k]].start()
            if 0 < order[k] < parts - 1:
                products[order[k] - 1].start()

    start_part(0)
    token[...] = jnp.zeros_like(token)
    width = TW + H

    def build(j, carry):
        mine = pl.ds(pl.multiple_of(j * TW, TW), TW)
        hots[j, 0] = hot(iota((width, TW), 0) == link_ref[2:3, mine] - j * TW)
        hots[j, 1] = hot(iota((width, TW), 0) == link_ref[3:4, mine] - (j * TW + H))
        return carry

    table[...] = got_ref[...].reshape(got_ref.shape[0], got_ref.shape[2]).T.astype(BF16)
    slots = table.shape[0] // 4
    for k in range(2):
        places[k].wait()
        pts = rim[k].astype(F32)
        east, north_, _, _ = winds_at(table[2 * k * slots : (2 * k + 1) * slots, :], pts[0:1], pts[1:2])
        rim_winds[0:1, k * H : (k + 1) * H] = east * pts[2:3]
        rim_winds[1:2, k * H : (k + 1) * H] = north_ * pts[2:3]
        rim_winds[2:3, k * H : (k + 1) * H] = pts[2:3]
    middle = points // TW // 2
    lax.fori_loop(0, middle, build, 0)
    start_part(1)
    matrix.start()
    lax.fori_loop(middle, points // TW, build, 0)
    low = iota((8, 128), 0) < 4

    def fill(i, lanes, mean, kinds):
        at = lane_tile(i)
        if kinds == "sn":
            air, over = winds_ref, lane_tile(i - per)
        else:
            air, over = rim_winds, at if kinds == "s" else lane_tile(i - points // 128)
        pattern = growth_pattern(tab_ref, air[0:1, over], air[1:2, over])
        msk = jnp.broadcast_to(air[2:3, over], (8, 128))
        quota = (0.15 * msk) * jnp.broadcast_to(mean / (1.0 + mean), (8, 128))
        wet = 0.5 * msk
        for m in range(NCH):
            rows = slice(m * CH, (m + 1) * CH)
            s = s_ref[rows, at].astype(F32)
            n = n_ref[rows, lane_tile(i - per)].astype(F32) if kinds == "sn" else product[rows, lanes]
            out = []
            for h in range(2):
                scale = step_scale(m, h)
                power = 1.21 ** (4 * m + 2 * h - NF / 2)
                near = msk - power * quota
                far = msk - (1.21 * power) * quota
                keeps = [near] * 4 + [jnp.where(low, near, far)] + [far] * 4
                for t, keep in enumerate(keeps):
                    tr = slice(8 * t, 8 * t + 8)
                    k = slice(HALF * h + 8 * t, HALF * h + 8 * t + 8)
                    grow = jnp.maximum(scale * pattern[tr] - 0.25, 0.0)
                    out.append(s[k] * (keep + grow) + n[k] * wet)
            x = jnp.concatenate(out, axis=0)
            natural[rows, at] = x.astype(BF16)
            picks = slice(m * 2 * PICK, (m + 1) * 2 * PICK)
            if "s" in kinds:
                south[picks, at] = chosen_rows(x, S_TILES)
            if "n" in kinds:
                north[picks, lane_tile(i - H // 128)] = chosen_rows(x, N_TILES)

    per = H // 128

    def fill_part(g, kinds):
        def own(i, carry):
            fill(i, slice(0, 128), mean_ref[0:1, lane_tile(i - per)], kinds)
            return carry

        if kinds == "sn":
            lax.fori_loop(g * per, (g + 1) * per, own, 0)
            return

        def body(q, carry):
            cols = pl.ds(pl.multiple_of(q * TW, TW), TW)
            product[...] = jnp.dot(it_ref[...], s_ref[:, cols], preferred_element_type=F32)
            acc = jnp.zeros((HALF, TW), F32)
            for m in range(NCH):
                s = s_ref[m * CH : (m + 1) * CH, cols].astype(F32)
                acc = acc + (s[:HALF] + s[HALF:])
            mean = jnp.sum(acc, axis=0, keepdims=True) * (1.0 / K)
            for l in range(TW // 128):
                lanes = slice(l * 128, (l + 1) * 128)
                fill(q * (TW // 128) + l, lanes, mean[:, lanes], kinds)
            return carry

        lax.fori_loop(g * (H // TW), (g + 1) * (H // TW), body, 0)

    def wait_part(k):
        loads[order[k]].wait()
        if 0 < order[k] < parts - 1:
            products[order[k] - 1].wait()
        start_part(k + 2)

    def output(j):
        window = pl.ds(pl.multiple_of(j * TW, TW), width)
        south_y[...] = jnp.dot(south[:, window], hots[j, 0], preferred_element_type=F32)
        north_y[...] = jnp.dot(north[:, window], hots[j, 1], preferred_element_type=F32)
        first = j * (TW // 128) + per
        for l in range(TW // 128):
            msk = winds_ref[2:3, lane_tile(first - per + l)]
            flows[l, 0] = tab_ref[2] * msk
            flows[l, 1] = tab_ref[3] * msk
        lane = iota((8, 128), 1)
        count = TW // 128
        for m in range(NCH):
            rows = slice(m * CH, (m + 1) * CH)
            near = [natural[rows, lane_tile(first + o - 1)].astype(F32) for o in range(count + 2)]
            ys = south_y[m * 2 * PICK : (m + 1) * 2 * PICK, :]
            yn = north_y[m * 2 * PICK : (m + 1) * 2 * PICK, :]
            out = [[] for _ in range(count)]
            for h in range(2):
                shrink = 1.1 ** (-(4 * m + 2 * h))
                for t in range(9):
                    at = slice(HALF * h + 8 * t, HALF * h + 8 * t + 8)
                    tr = slice(8 * t, 8 * t + 8)
                    kind = west_kind(t)
                    tile = [n[at] for n in near]
                    if kind != "east":
                        ahead = [pltpu.roll(x, 1, 1) for x in tile[:-1]]
                    if kind != "west":
                        behind = [pltpu.roll(x, 127, 1) for x in tile[1:]]
                    for l in range(count):
                        c = tile[l + 1]
                        if kind != "east":
                            x = west = jnp.where(lane == 0, ahead[l], ahead[l + 1])
                        if kind != "west":
                            x = east = jnp.where(lane == 127, behind[l + 1], behind[l])
                        if kind == "both":
                            x = jnp.where(tab_ref[5, tr] > 0, west, east)
                        lanes = slice(l * 128, (l + 1) * 128)
                        if t in S_TILES:
                            k = PICK * h + 8 * S_TILES.index(t)
                            y = ys[k : k + 8, lanes]
                        if t in N_TILES:
                            k = PICK * h + 8 * N_TILES.index(t)
                            z = yn[k : k + 8, lanes]
                            y = jnp.where(tab_ref[6, tr] > 0, y, z) if t in S_TILES else z
                        flow = flows[l, 0, tr] * x + flows[l, 1, tr] * y - tab_ref[4, tr] * c
                        out[l].append(c + shrink * flow)
            for l in range(count):
                staged[rows, lane_tile(j * count + l)] = jnp.concatenate(out[l], axis=0).astype(BF16)

    def stores(j):
        at = pl.ds(j * TW, TW)
        return pltpu.make_async_copy(staged.at[:, at], out_hbm.at[:, at], sems.at[2 * parts + 1 + j])

    pair = H // TW
    wait_part(0)
    fill_part(1, "sn")
    wait_part(1)
    matrix.wait()
    fill_part(0, "s")
    for g in range(2, parts):
        wait_part(g)
        fill_part(g, "n" if g == parts - 1 else "sn")
        lax.fori_loop((g - 2) * pair, (g - 1) * pair, lambda j, c: (output(j), c)[1], 0)
        for j in range((g - 2) * pair, (g - 1) * pair):
            stores(j).start()
    for j in range(points // TW):
        stores(j).wait()


def move(tab, winds, links, got, mean, interact, spectra, before, after, nonlinear):
    points = links.shape[1]
    extended = points + 2 * H
    return pl.pallas_call(
        move_kernel,
        in_specs=[HERE] * 5 + [AWAY] * 5,
        out_specs=[AWAY, HERE],
        out_shape=[jax.ShapeDtypeStruct((K, points), BF16), jax.ShapeDtypeStruct((8, 128), F32)],
        scratch_shapes=[
            pltpu.VMEM((got.shape[2], got.shape[0]), BF16),
            pltpu.VMEM((2, 16, H), BF16),
            pltpu.VMEM((8, 2 * H), F32),
            pltpu.VMEM((K, K), BF16),
            pltpu.VMEM((K, extended), BF16),
            pltpu.VMEM((K, points), BF16),
            pltpu.VMEM((K, TW), F32),
            pltpu.VMEM((K, extended), BF16),
            pltpu.VMEM((18 * PICK, points + H), BF16),
            pltpu.VMEM((18 * PICK, points + H), BF16),
            pltpu.VMEM((K, points), BF16),
            pltpu.VMEM((points // TW, 2, TW + H, TW), BF16),
            pltpu.VMEM((18 * PICK, TW), F32),
            pltpu.VMEM((18 * PICK, TW), F32),
            pltpu.VMEM((TW // 128, 2, HALF, 128), F32),
            pltpu.SemaphoreType.DMA((2 * (points // H + 2) + 1 + points // TW,)),
        ],
        compiler_params=params(BIG),
        cost_estimate=cost(2 * 2 * 18 * PICK * (TW + H) * points + 2 * K * K * extended, K * points * 8),
        name="move",
    )(tab, winds, links, got, mean, interact, spectra, before, after, nonlinear)


def cell_kernel(got_ref, push_ref, pusht_ref, air_ref, wait_ref, wind_ref, rough_ref, left, right):
    capacity, blocks = pusht_ref.shape
    lat_dev = air_ref.shape[1]
    values = got_ref[...].reshape(blocks, 4 * capacity).T
    high = values.astype(BF16).astype(F32)
    low = values - high
    for r in range(capacity):
        cols = slice(r * blocks, (r + 1) * blocks)
        at_row = iota((lat_dev, blocks), 0) == (pusht_ref[r : r + 1, :] >> 7)
        for part, source in enumerate((high, low)):
            rows = [
                jnp.where(at_row, source[c * capacity + r : c * capacity + r + 1, :], 0.0) for c in range(4)
            ]
            left[part * 4 * lat_dev : (part + 1) * 4 * lat_dev, cols] = jnp.concatenate(rows, axis=0).astype(BF16)
        right[cols, :] = hot(iota((blocks, 128), 1) == (push_ref[:, r : r + 1] & 127))
    sums = jnp.dot(left[...], right[...], preferred_element_type=F32)
    sums = sums[: 4 * lat_dev] + sums[4 * lat_dev :]
    sx, sy, rough, share = (sums[c * lat_dev : (c + 1) * lat_dev] for c in range(4))
    count = jnp.maximum(share, 1.0)
    wind_ref[0] = air_ref[0] - 0.5 * (sx / count)
    wind_ref[1] = air_ref[1] - 0.5 * (sy / count)
    rough_ref[...] = rough / count


def cells(got, push, pusht, air_state, wait):
    capacity, blocks = pusht.shape
    lat_dev = air_state.shape[1]
    return pl.pallas_call(
        cell_kernel,
        in_specs=[HERE] * 4 + [AWAY],
        out_specs=[HERE] * 2,
        out_shape=[
            jax.ShapeDtypeStruct(air_state.shape, F32),
            jax.ShapeDtypeStruct(air_state.shape[1:], F32),
        ],
        scratch_shapes=[
            pltpu.VMEM((8 * lat_dev, capacity * blocks), BF16),
            pltpu.VMEM((capacity * blocks, 128), BF16),
        ],
        compiler_params=params(BIG),
        cost_estimate=cost(2 * 8 * lat_dev * 128 * capacity * blocks, 400000),
        name="cells",
    )(got, push, pusht, air_state, wait)


def chain(axis, step):
    peers = lax.axis_size(axis)
    pairs = [(i, i + 1) for i in range(peers - 1)]
    return pairs if step > 0 else [(j, i) for i, j in pairs]


def shards(spectra, interact, sea_mask, sea_tile, push_list, neighbors, air_wind, diffusion):
    both = ("wave", "atm")
    tab = jnp.asarray(row_tables())
    lat_total = air_wind.shape[1] * lax.axis_size("atm")
    points = spectra.shape[1]
    push = push_list[0]

    pack = jnp.concatenate([air_wind, diffusion[None]], axis=0)
    above = lax.ppermute(pack[:, -8:], "atm", chain("atm", 1))
    below = lax.ppermute(pack[:, :8], "atm", chain("atm", -1))
    mid = jnp.concatenate([above, pack, below], axis=1)
    pts, pusht, to_prev, to_next = prepare(jnp.stack([sea_tile, sea_mask]), push, spectra)
    mid, pts, pusht, to_prev, to_next = lax.optimization_barrier((mid, pts, pusht, to_prev, to_next))
    left = lax.ppermute(mid, "wave", chain("wave", 1))
    right = lax.ppermute(mid, "wave", chain("wave", -1))


    air_state, outgoing = air(lat_total, mid, left, right, pusht)
    outgoing, to_prev, to_next = lax.optimization_barrier((outgoing, to_prev, to_next))
    arrived = lax.all_to_all(outgoing, both, split_axis=0, concat_axis=0, tiled=True)
    before = lax.ppermute(to_next, both, chain(both, 1))
    after = lax.ppermute(to_prev, both, chain(both, -1))
    nonlinear, mean = interactions(interact, [spectra], points, outgoing, "interact_own")
    outbound, winds = stresses(tab, arrived, pts, spectra, mean)
    inbound = lax.all_to_all(outbound, both, split_axis=0, concat_axis=0, tiled=True)
    wave_spectra, token = move(tab, winds, neighbors, arrived, mean, interact, spectra, before, after, nonlinear)
    surface_wind, roughness = cells(inbound, push, pusht, air_state, token)
    return (wave_spectra, surface_wind, roughness)


def solution(mesh):
    placed = (
        P(None, ("wave", "atm")),
        P(),
        P(("wave", "atm")),
        P(("wave", "atm")),
        P(("wave", "atm"), None, None),
        P(None, ("wave", "atm")),
        P(None, "atm", "wave"),
        P("atm", "wave"),
    )
    return jax.shard_map(
        shards,
        mesh=mesh,
        in_specs=placed,
        out_specs=(P(None, ("wave", "atm")), P(None, "atm", "wave"), P("atm", "wave")),
        check_vma=False,
    )
```

time: 100 us -> 98.7 us (0.987)
  Pallas kernels: 55.6 us -> 51.4 us
  starting transfers between devices: 39.1 us -> 41.6 us
  local copies, waits for them, and re-layouts: 2.22 us -> 0.84 us
    pallas_call x6 -> x5, Pallas kernels: 53.1 us -> 48.9 us  [the longest x1 24.5 us: move(): pl.pallas_call(move_kernel, in_specs=[HERE] * 5 + [AWAY] * 5, out_specs=[...]
    ppermute x1, waiting for transfers between devices: 0.01 us -> 1.52 us  [shards(): left = lax.ppermute(mid, 'wave', chain('wave', 1))]
    ppermute x1, starting transfers between devices: 3.64 us -> 5.08 us  [shards(): before = lax.ppermute(to_next, both, chain(both, 1))]
    unnamed x13 -> x9, local copies, waits for them, and re-layouts: 2.22 us -> 0.84 us
  transfers between devices with their start and end apart: 8 -> 8, of which waited for: 1 -> 2; matrix products, arithmetic and copies ran while one was open for 1% -> 2% of each run, Pallas kernels for 48% -> 48%
where the time goes in v2:
time: 98.7 us; the launch traced here: 98 us
  Pallas kernels  51.4 us (52%)
  starting transfers between devices  41.6 us (42%)
  waiting for transfers between devices  1.86 us (2%)
  other arithmetic  1.53 us (2%)
    pallas_call x1, Pallas kernels, move(): pl.pallas_call(move_kernel, in_specs=[HERE] * 5 + [AWAY] * 5, out_specs=[...  24.5 us
    pallas_call x1, Pallas kernels, interactions(): pl.pallas_call(interact_kernel, in_specs=[AWAY] * (len(sources) + 2), out...  14 us
    all_to_all x1, starting transfers between devices, shards(): lax.all_to_all(outgoing, both, split_axis=0, concat_axis=0, tiled=True)  12.7 us
    all_to_all x1, starting transfers between devices, shards(): lax.all_to_all(outbound, both, split_axis=0, concat_axis=0, tiled=True)  9.77 us
    pallas_call x1, Pallas kernels, stresses(): pl.pallas_call(stress_kernel, in_specs=[HERE] * 3 + [AWAY] * 2, out_specs...  5.34 us
    ppermute x1, starting transfers between devices, shards(): before = lax.ppermute(to_next, both, chain(both, 1))  5.08 us
    ppermute x1, starting transfers between devices, shards(): above = lax.ppermute(pack[:, -8:], 'atm', chain('atm', 1))  4.92 us
    ppermute x1, starting transfers between devices, shards(): left = lax.ppermute(mid, 'wave', chain('wave', 1))  3.99 us
  transfers between devices with their start and end apart: 8, of which 2 were waited for; matrix products, arithmetic and copies ran while one was open for 2% of the time, Pallas kernels for 48%

profile of v2, /device:TPU:1, one launch (start us, length us, event | category | flops | bytes accessed | tf_op | source)
XLA Modules:
  0.0 98.0 jit_solution(8833493137180442609)
XLA Ops:
  0.7 0.8 pad_maximum_fusion.2
  1.4 4.9 %collective-permute-start = (f32[3,8,128]{2,1,0:T(8,128)S(1)}, f32[3,8,128]{2,1,0:T(8,128)S(1)}, u32[]{:S(2)}, u32[]{:S(2)}) collective-permute-start(f32[3,8,128]{2,1,0:T(8,128)S(1)} %get-tuple-element.47), channel_id=1, source_target_pairs={{0,1},{1,2},{2,3},{3,4},{4,5},{5,6},{6,7},{8,9},{9,10},{10,11},{11... | collective-permute-start | bytes 36872 | tf_op jit(solution)/shard_map/ppermute | solution.py:697
  6.4 1.9 %collective-permute-start.1 = (f32[3,8,128]{2,1,0:T(8,128)S(1)}, f32[3,8,128]{2,1,0:T(8,128)S(1)}, u32[]{:S(2)}, u32[]{:S(2)}) collective-permute-start(f32[3,8,128]{2,1,0:T(8,128)S(1)} %get-tuple-element.48), channel_id=1, source_target_pairs={{1,0},{2,1},{3,2},{4,3},{5,4},{6,5},{7,6},{9,8},{10,9},{11,10},{12... | collective-permute-start | bytes 36872 | tf_op jit(solution)/shard_map/ppermute | solution.py:698
  8.3 0.8 copy.12
  9.1 0.7 pad_add_fusion.code_ref
  9.8 2.8 %prepare.1 = (f32[8,2048]{1,0:T(8,128)S(1)}, s32[32,128]{1,0:T(8,128)S(1)}, bf16[1312,512]{1,0:T(8,128)(2,1)S(1)}, bf16[1312,512]{1,0:T(8,128)(2,1)}) custom-call(s32[2,2048]{1,0:T(2,128)S(1)} %pad_add_fusion.code_ref, s32[128,32]{1,0:T(8,128)S(1)} %bitcast.4, bf16[1296,2048]{1,0:T(8,128)(2,1)} %s_hbm.3), custom_call_target="tpu_custom_call" | custom-call | flops 268435456 | bytes 5373952 | tf_op jit(solution)/shard_map/prepare/pallas_call | solution.py:126
  12.7 0.0 collective-permute-done
  12.7 0.0 collective-permute-done.1
  12.8 1.3 %collective-permute-start.3 = (f32[3,80,128]{2,1,0:T(8,128)S(1)}, f32[3,80,128]{2,1,0:T(8,128)S(1)}, u32[]{:S(2)}, u32[]{:S(2)}) collective-permute-start(f32[3,80,128]{2,1,0:T(8,128)S(1)} %pad_maximum_fusion.refs_0_), channel_id=1, source_target_pairs={{8,0},{16,8},{24,16},{32,24},{40,32},{48,40},{56,48},{64,56},{72,6... | collective-permute-start | bytes 368648 | tf_op jit(solution)/shard_map/ppermute | solution.py:703
  14.1 4.0 %collective-permute-start.2 = (f32[3,80,128]{2,1,0:T(8,128)S(1)}, f32[3,80,128]{2,1,0:T(8,128)S(1)}, u32[]{:S(2)}, u32[]{:S(2)}) collective-permute-start(f32[3,80,128]{2,1,0:T(8,128)S(1)} %pad_maximum_fusion.refs_0_), channel_id=1, source_target_pairs={{0,8},{8,16},{16,24},{24,32},{32,40},{40,48},{48,56},{56,64},{64,7... | collective-permute-start | bytes 368648 | tf_op jit(solution)/shard_map/ppermute | solution.py:702
  18.1 0.3 collective-permute-done.3.refs_2_
  18.4 1.5 %collective-permute-done.2.refs_1_ = f32[3,80,128]{2,1,0:T(8,128)S(1)} collective-permute-done((f32[3,80,128]{2,1,0:T(8,128)S(1)}, f32[3,80,128]{2,1,0:T(8,128)S(1)}, u32[]{:S(2)}, u32[]{:S(2)}) %collective-permute-start.2) | collective-permute-done | bytes 122912 | tf_op jit(solution)/shard_map/ppermute | solution.py:702
  19.9 2.2 %air.1 = (f32[2,64,128]{2,1,0:T(8,128)S(1)}, f32[128,1,256]{2,1,0:T(1,128)}) custom-call(f32[3,80,128]{2,1,0:T(8,128)S(1)} %pad_maximum_fusion.refs_0_, f32[3,80,128]{2,1,0:T(8,128)S(1)} %collective-permute-done.2.refs_1_, f32[3,80,128]{2,1,0:T(8,128)S(1)} %collective-permute-done.3.refs_2_, s32[32,128]{1,0:T(8,128)S(1)} %get-tuple-element.30.refs_3_.pusht_ref), custom_call_target="tpu_custom_call" | custom-call | flops 134217728 | bytes 600000 | tf_op jit(solution)/shard_map/air/pallas_call | solution.py:272
  22.1 5.1 %collective-permute-start.4 = (bf16[1312,512]{1,0:T(8,128)(2,1)}, bf16[1312,512]{1,0:T(8,128)(2,1)S(1)}, u32[]{:S(2)}, u32[]{:S(2)}) collective-permute-start(bf16[1312,512]{1,0:T(8,128)(2,1)} %get-tuple-element.38), channel_id=1, source_target_pairs={{0,1},{1,2},{2,3},{3,4},{4,5},{5,6},{6,7},{7,8},{8,9},{9,10},{10,1... | collective-permute-start | bytes 4030472 | tf_op jit(solution)/shard_map/ppermute | solution.py:709
  27.1 1.9 %collective-permute-start.5 = (bf16[1312,512]{1,0:T(8,128)(2,1)S(1)}, bf16[1312,512]{1,0:T(8,128)(2,1)}, u32[]{:S(2)}, u32[]{:S(2)}) collective-permute-start(bf16[1312,512]{1,0:T(8,128)(2,1)S(1)} %get-tuple-element.39), channel_id=1, source_target_pairs={{1,0},{2,1},{3,2},{4,3},{5,4},{6,5},{7,6},{8,7},{9,8},{10,9},{11,1... | collective-permute-start | bytes 4030472 | tf_op jit(solution)/shard_map/ppermute | solution.py:710
  29.1 12.7 %all-to-all-start = ((f32[128,1,256]{2,1,0:T(1,128)}), f32[128,1,256]{2,1,0:T(1,128)S(1)}, u32[]{:S(2)}, u32[]{:S(2)}) async-start(f32[128,1,256]{2,1,0:T(1,128)} %get-tuple-element.34.refs_1_), calls=%async_computation | async-start | bytes 262144 | tf_op jit(solution)/shard_map/all_to_all | solution.py:708
  41.8 0.0 copy-start
  41.8 14.0 %interact_own.1 = (bf16[1296,2048]{1,0:T(8,128)(2,1)}, f32[8,2048]{1,0:T(8,128)S(1)}) custom-call(bf16[1296,1296]{1,0:T(8,128)(2,1)} %it_hbm.3, bf16[1296,2048]{1,0:T(8,128)(2,1)} %s_hbm.3, f32[128,1,256]{2,1,0:T(1,128)} %get-tuple-element.34.refs_1_), custom_call_target="tpu_custom_call" | custom-call | flops 6879707136 | bytes 10616832 | tf_op jit(solution)/shard_map/interact_own/pallas_call | solution.py:207
  55.8 0.0 copy-start.1
  55.9 0.0 all-to-all-done.got_ref
  55.9 5.3 %stress.1 = (f32[128,1,128]{2,1,0:T(1,128)}, f32[8,2048]{1,0:T(8,128)S(1)}) custom-call(f32[7,72,128]{2,1,0:T(8,128)S(1)} %copy-done, f32[128,1,256]{2,1,0:T(1,128)S(1)} %all-to-all-done.got_ref, f32[8,2048]{1,0:T(8,128)S(1)} %get-tuple-element.35.p_ref, bf16[1296,2048]{1,0:T(8,128)(2,1)} %s_hbm.3, f32[8,2048]{1,0:T(8,128)S(1)} %get-tuple-element.36.wait_ref.mean_ref), custom_call_target="tpu_custom_call" | custom-call | flops 26542080 | bytes 5308416 | tf_op jit(solution)/shard_map/stress/pallas_call | solution.py:384
  61.2 9.8 %all-to-all-start.1 = ((f32[128,1,128]{2,1,0:T(1,128)}), f32[128,1,128]{2,1,0:T(1,128)S(1)}, u32[]{:S(2)}, u32[]{:S(2)}) async-start(f32[128,1,128]{2,1,0:T(1,128)} %get-tuple-element.42), calls=%async_computation.1 | async-start | bytes 131072 | tf_op jit(solution)/shard_map/all_to_all | solution.py:713
  71.0 24.5 %move.1 = (bf16[1296,2048]{1,0:T(8,128)(2,1)}, f32[8,128]{1,0:T(8,128)S(1)}) custom-call(f32[7,72,128]{2,1,0:T(8,128)S(1)} %copy-done, f32[8,2048]{1,0:T(8,128)S(1)} %get-tuple-element.37.winds_ref, s32[4,2048]{1,0:T(4,128)S(1)} %copy-done.1, f32[128,1,256]{2,1,0:T(1,128)S(1)} %all-to-all-done.got_ref, f32[8,2048]{1,0:T(8,128)S(1)} %get-tuple-element.36.wait_ref.mean_ref, ...), custom_call_target="tpu_custom_call" | custom-call | flops 15755378688 | bytes 21233664 | tf_op jit(solution)/shard_map/move/pallas_call | solution.py:609
  95.6 2.4 %cells.1 = (f32[2,64,128]{2,1,0:T(8,128)}, f32[64,128]{1,0:T(8,128)}) custom-call(f32[128,1,128]{2,1,0:T(1,128)S(1)} %all-to-all-done.1.got_ref, s32[128,32]{1,0:T(8,128)S(1)} %bitcast.5, s32[32,128]{1,0:T(8,128)S(1)} %get-tuple-element.30.refs_3_.pusht_ref, f32[2,64,128]{2,1,0:T(8,128)S(1)} %get-tuple-element.43.air_ref, ...), custom_call_target="tpu_custom_call" | custom-call | flops 536870912 | bytes 400000 | tf_op jit(solution)/shard_map/cells/pallas_call | solution.py:665
  (10 shorter events, 0.0 us)
Async XLA Ops:
  0.6 12.1 %copy-start.2 = (f32[2,64,128]{2,1,0:T(8,128)S(1)}, f32[2,64,128]{2,1,0:T(8,128)}, u32[]{:S(2)}) copy-start(f32[2,64,128]{2,1,0:T(8,128)} %param.15) | copy-start | bytes 196612
  0.6 12.1 %copy-start.3 = (f32[64,128]{1,0:T(8,128)S(1)}, f32[64,128]{1,0:T(8,128)}, u32[]{:S(2)}) copy-start(f32[64,128]{1,0:T(8,128)} %param.16) | copy-start | bytes 98308
  1.4 11.3 %collective-permute-start = (f32[3,8,128]{2,1,0:T(8,128)S(1)}, f32[3,8,128]{2,1,0:T(8,128)S(1)}, u32[]{:S(2)}, u32[]{:S(2)}) collective-permute-start(f32[3,8,128]{2,1,0:T(8,128)S(1)} %get-tuple-element.47), channel_id=1, source_target_pairs={{0,1},{1,2},{2,3},{3,4},{4,5},{5,6},{6,7},{8,9},{9,10},{10,11},{11... | collective-permute-start | bytes 36872 | tf_op jit(solution)/shard_map/ppermute | solution.py:697
  6.4 6.3 %collective-permute-start.1 = (f32[3,8,128]{2,1,0:T(8,128)S(1)}, f32[3,8,128]{2,1,0:T(8,128)S(1)}, u32[]{:S(2)}, u32[]{:S(2)}) collective-permute-start(f32[3,8,128]{2,1,0:T(8,128)S(1)} %get-tuple-element.48), channel_id=1, source_target_pairs={{1,0},{2,1},{3,2},{4,3},{5,4},{6,5},{7,6},{9,8},{10,9},{11,10},{12... | collective-permute-start | bytes 36872 | tf_op jit(solution)/shard_map/ppermute | solution.py:698
  12.8 5.6 %collective-permute-start.3 = (f32[3,80,128]{2,1,0:T(8,128)S(1)}, f32[3,80,128]{2,1,0:T(8,128)S(1)}, u32[]{:S(2)}, u32[]{:S(2)}) collective-permute-start(f32[3,80,128]{2,1,0:T(8,128)S(1)} %pad_maximum_fusion.refs_0_), channel_id=1, source_target_pairs={{8,0},{16,8},{24,16},{32,24},{40,32},{48,40},{56,48},{64,56},{72,6... | collective-permute-start | bytes 368648 | tf_op jit(solution)/shard_map/ppermute | solution.py:703
  14.1 5.8 %collective-permute-start.2 = (f32[3,80,128]{2,1,0:T(8,128)S(1)}, f32[3,80,128]{2,1,0:T(8,128)S(1)}, u32[]{:S(2)}, u32[]{:S(2)}) collective-permute-start(f32[3,80,128]{2,1,0:T(8,128)S(1)} %pad_maximum_fusion.refs_0_), channel_id=1, source_target_pairs={{0,8},{8,16},{16,24},{24,32},{32,40},{40,48},{48,56},{56,64},{64,7... | collective-permute-start | bytes 368648 | tf_op jit(solution)/shard_map/ppermute | solution.py:702
  22.1 49.0 %collective-permute-start.4 = (bf16[1312,512]{1,0:T(8,128)(2,1)}, bf16[1312,512]{1,0:T(8,128)(2,1)S(1)}, u32[]{:S(2)}, u32[]{:S(2)}) collective-permute-start(bf16[1312,512]{1,0:T(8,128)(2,1)} %get-tuple-element.38), channel_id=1, source_target_pairs={{0,1},{1,2},{2,3},{3,4},{4,5},{5,6},{6,7},{7,8},{8,9},{9,10},{10,1... | collective-permute-start | bytes 4030472 | tf_op jit(solution)/shard_map/ppermute | solution.py:709
  27.1 43.9 %collective-permute-start.5 = (bf16[1312,512]{1,0:T(8,128)(2,1)S(1)}, bf16[1312,512]{1,0:T(8,128)(2,1)}, u32[]{:S(2)}, u32[]{:S(2)}) collective-permute-start(bf16[1312,512]{1,0:T(8,128)(2,1)S(1)} %get-tuple-element.39), channel_id=1, source_target_pairs={{1,0},{2,1},{3,2},{4,3},{5,4},{6,5},{7,6},{8,7},{9,8},{10,9},{11,1... | collective-permute-start | bytes 4030472 | tf_op jit(solution)/shard_map/ppermute | solution.py:710
  29.1 26.8 %all-to-all-start = ((f32[128,1,256]{2,1,0:T(1,128)}), f32[128,1,256]{2,1,0:T(1,128)S(1)}, u32[]{:S(2)}, u32[]{:S(2)}) async-start(f32[128,1,256]{2,1,0:T(1,128)} %get-tuple-element.34.refs_1_), calls=%async_computation | async-start | bytes 262144 | tf_op jit(solution)/shard_map/all_to_all | solution.py:708
  41.8 14.1 %copy-start = (f32[7,72,128]{2,1,0:T(8,128)S(1)}, f32[7,72,128]{2,1,0:T(8,128)}, u32[]{:S(2)}) copy-start(f32[7,72,128]{2,1,0:T(8,128)} %constant.2.clone.tab_ref) | copy-start | bytes 774148
  55.8 15.2 %copy-start.1 = (s32[4,2048]{1,0:T(4,128)S(1)}, s32[4,2048]{1,0:T(4,128)}, u32[]{:S(2)}) copy-start(s32[4,2048]{1,0:T(4,128)} %link_ref.1) | copy-start | bytes 98308
  61.2 34.4 %all-to-all-start.1 = ((f32[128,1,128]{2,1,0:T(1,128)}), f32[128,1,128]{2,1,0:T(1,128)S(1)}, u32[]{:S(2)}, u32[]{:S(2)}) async-start(f32[128,1,128]{2,1,0:T(1,128)} %get-tuple-element.42), calls=%async_computation.1 | async-start | bytes 131072 | tf_op jit(solution)/shard_map/all_to_all | solution.py:713

commit v3 on v2

--- a/solution.py
+++ b/solution.py
@@ -166,6 +166,9 @@
     def store(i):
         return pltpu.make_async_copy(out_ref.at[i], out_hbm.at[:, columns(i)], sems.at[tiles + parts + i])
 
+    def load_at(i):
+        return pltpu.make_async_copy(sources[0].at[pl.ds(0, K), columns(i)], s_ref.at[i], sems.at[i])
+
     def mean_of(i):
         acc = jnp.zeros((HALF, TW), F32)
         for m in range(NCH):
@@ -185,13 +188,16 @@
         pieces[c].wait()
         if c == 0:
             pieces[3].start()
+            load_at(2).start()
         out_ref[0, a:b, :] = jnp.dot(it_ref[a:b, :], s_ref[0], preferred_element_type=F32).astype(BF16)
     store(0).start()
-    for load in loads[2:]:
-        load.start()
 
     def body(i, carry):
-        pltpu.make_async_copy(sources[0].at[pl.ds(0, K), pl.ds(0, TW)], s_ref.at[i], sems.at[i]).wait()
+        @pl.when(i + 2 < tiles)
+        def _():
+            load_at(i + 2).start()
+
+        load_at(i).wait()
         out_ref[i] = jnp.dot(it_ref[...], s_ref[i], preferred_element_type=F32).astype(BF16)
         store(i).start()
         mean_of(i)
@@ -584,7 +590,7 @@
                 staged[rows, lane_tile(j * count + l)] = jnp.concatenate(out[l], axis=0).astype(BF16)
 
     def stores(j):
-        at = pl.ds(j * TW, TW)
+        at = columns(j)
         return pltpu.make_async_copy(staged.at[:, at], out_hbm.at[:, at], sems.at[2 * parts + 1 + j])
 
     pair = H // TW
@@ -596,9 +602,7 @@
     for g in range(2, parts):
         wait_part(g)
         fill_part(g, "n" if g == parts - 1 else "sn")
-        lax.fori_loop((g - 2) * pair, (g - 1) * pair, lambda j, c: (output(j), c)[1], 0)
-        for j in range((g - 2) * pair, (g - 1) * pair):
-            stores(j).start()
+        lax.fori_loop((g - 2) * pair, (g - 1) * pair, lambda j, c: (output(j), stores(j).start(), c)[2], 0)
     for j in range(points // TW):
         stores(j).wait()
 

time: 98.7 us -> 98.4 us (level)
  no operation moved by 1% of the time
where the time goes in v3:
time: 98.4 us; the launch traced here: 97.8 us
  Pallas kernels  51.1 us (52%)
  starting transfers between devices  41.6 us (42%)
  waiting for transfers between devices  1.86 us (2%)
  other arithmetic  1.53 us (2%)
    pallas_call x1, Pallas kernels, move(): pl.pallas_call(move_kernel, in_specs=[HERE] * 5 + [AWAY] * 5, out_specs=[...  24.3 us
    pallas_call x1, Pallas kernels, interactions(): pl.pallas_call(interact_kernel, in_specs=[AWAY] * (len(sources) + 2), out...  14 us
    all_to_all x1, starting transfers between devices, shards(): lax.all_to_all(outgoing, both, split_axis=0, concat_axis=0, tiled=True)  12.7 us
    all_to_all x1, starting transfers between devices, shards(): lax.all_to_all(outbound, both, split_axis=0, concat_axis=0, tiled=True)  9.77 us
    pallas_call x1, Pallas kernels, stresses(): pl.pallas_call(stress_kernel, in_specs=[HERE] * 3 + [AWAY] * 2, out_specs...  5.34 us
    ppermute x1, starting transfers between devices, shards(): before = lax.ppermute(to_next, both, chain(both, 1))  5.08 us
    ppermute x1, starting transfers between devices, shards(): above = lax.ppermute(pack[:, -8:], 'atm', chain('atm', 1))  4.92 us
    ppermute x1, starting transfers between devices, shards(): left = lax.ppermute(mid, 'wave', chain('wave', 1))  3.99 us
  transfers between devices with their start and end apart: 8, of which 2 were waited for; matrix products, arithmetic and copies ran while one was open for 2% of the time, Pallas kernels for 48%

profile of v3, /device:TPU:1, one launch (start us, length us, event | category | flops | bytes accessed | tf_op | source)
XLA Modules:
  0.0 97.8 jit_solution(10618255631797552784)
XLA Ops:
  0.7 0.8 pad_maximum_fusion.2
  1.4 4.9 %collective-permute-start = (f32[3,8,128]{2,1,0:T(8,128)S(1)}, f32[3,8,128]{2,1,0:T(8,128)S(1)}, u32[]{:S(2)}, u32[]{:S(2)}) collective-permute-start(f32[3,8,128]{2,1,0:T(8,128)S(1)} %get-tuple-element.47), channel_id=1, source_target_pairs={{0,1},{1,2},{2,3},{3,4},{4,5},{5,6},{6,7},{8,9},{9,10},{10,11},{11... | collective-permute-start | bytes 36872 | tf_op jit(solution)/shard_map/ppermute | solution.py:701
  6.4 1.9 %collective-permute-start.1 = (f32[3,8,128]{2,1,0:T(8,128)S(1)}, f32[3,8,128]{2,1,0:T(8,128)S(1)}, u32[]{:S(2)}, u32[]{:S(2)}) collective-permute-start(f32[3,8,128]{2,1,0:T(8,128)S(1)} %get-tuple-element.48), channel_id=1, source_target_pairs={{1,0},{2,1},{3,2},{4,3},{5,4},{6,5},{7,6},{9,8},{10,9},{11,10},{12... | collective-permute-start | bytes 36872 | tf_op jit(solution)/shard_map/ppermute | solution.py:702
  8.3 0.8 copy.12
  9.1 0.7 pad_add_fusion.code_ref
  9.8 2.8 %prepare.1 = (f32[8,2048]{1,0:T(8,128)S(1)}, s32[32,128]{1,0:T(8,128)S(1)}, bf16[1312,512]{1,0:T(8,128)(2,1)S(1)}, bf16[1312,512]{1,0:T(8,128)(2,1)}) custom-call(s32[2,2048]{1,0:T(2,128)S(1)} %pad_add_fusion.code_ref, s32[128,32]{1,0:T(8,128)S(1)} %bitcast.4, bf16[1296,2048]{1,0:T(8,128)(2,1)} %s_hbm.3), custom_call_target="tpu_custom_call" | custom-call | flops 268435456 | bytes 5373952 | tf_op jit(solution)/shard_map/prepare/pallas_call | solution.py:126
  12.7 0.0 collective-permute-done
  12.7 0.0 collective-permute-done.1
  12.8 1.3 %collective-permute-start.3 = (f32[3,80,128]{2,1,0:T(8,128)S(1)}, f32[3,80,128]{2,1,0:T(8,128)S(1)}, u32[]{:S(2)}, u32[]{:S(2)}) collective-permute-start(f32[3,80,128]{2,1,0:T(8,128)S(1)} %pad_maximum_fusion.refs_0_), channel_id=1, source_target_pairs={{8,0},{16,8},{24,16},{32,24},{40,32},{48,40},{56,48},{64,56},{72,6... | collective-permute-start | bytes 368648 | tf_op jit(solution)/shard_map/ppermute | solution.py:707
  14.1 4.0 %collective-permute-start.2 = (f32[3,80,128]{2,1,0:T(8,128)S(1)}, f32[3,80,128]{2,1,0:T(8,128)S(1)}, u32[]{:S(2)}, u32[]{:S(2)}) collective-permute-start(f32[3,80,128]{2,1,0:T(8,128)S(1)} %pad_maximum_fusion.refs_0_), channel_id=1, source_target_pairs={{0,8},{8,16},{16,24},{24,32},{32,40},{40,48},{48,56},{56,64},{64,7... | collective-permute-start | bytes 368648 | tf_op jit(solution)/shard_map/ppermute | solution.py:706
  18.1 0.3 collective-permute-done.3.refs_2_
  18.4 1.5 %collective-permute-done.2.refs_1_ = f32[3,80,128]{2,1,0:T(8,128)S(1)} collective-permute-done((f32[3,80,128]{2,1,0:T(8,128)S(1)}, f32[3,80,128]{2,1,0:T(8,128)S(1)}, u32[]{:S(2)}, u32[]{:S(2)}) %collective-permute-start.2) | collective-permute-done | bytes 122912 | tf_op jit(solution)/shard_map/ppermute | solution.py:706
  19.9 2.2 %air.1 = (f32[2,64,128]{2,1,0:T(8,128)S(1)}, f32[128,1,256]{2,1,0:T(1,128)}) custom-call(f32[3,80,128]{2,1,0:T(8,128)S(1)} %pad_maximum_fusion.refs_0_, f32[3,80,128]{2,1,0:T(8,128)S(1)} %collective-permute-done.2.refs_1_, f32[3,80,128]{2,1,0:T(8,128)S(1)} %collective-permute-done.3.refs_2_, s32[32,128]{1,0:T(8,128)S(1)} %get-tuple-element.30.refs_3_.pusht_ref), custom_call_target="tpu_custom_call" | custom-call | flops 134217728 | bytes 600000 | tf_op jit(solution)/shard_map/air/pallas_call | solution.py:278
  22.1 5.1 %collective-permute-start.4 = (bf16[1312,512]{1,0:T(8,128)(2,1)}, bf16[1312,512]{1,0:T(8,128)(2,1)S(1)}, u32[]{:S(2)}, u32[]{:S(2)}) collective-permute-start(bf16[1312,512]{1,0:T(8,128)(2,1)} %get-tuple-element.38), channel_id=1, source_target_pairs={{0,1},{1,2},{2,3},{3,4},{4,5},{5,6},{6,7},{7,8},{8,9},{9,10},{10,1... | collective-permute-start | bytes 4030472 | tf_op jit(solution)/shard_map/ppermute | solution.py:713
  27.1 1.9 %collective-permute-start.5 = (bf16[1312,512]{1,0:T(8,128)(2,1)S(1)}, bf16[1312,512]{1,0:T(8,128)(2,1)}, u32[]{:S(2)}, u32[]{:S(2)}) collective-permute-start(bf16[1312,512]{1,0:T(8,128)(2,1)S(1)} %get-tuple-element.39), channel_id=1, source_target_pairs={{1,0},{2,1},{3,2},{4,3},{5,4},{6,5},{7,6},{8,7},{9,8},{10,9},{11,1... | collective-permute-start | bytes 4030472 | tf_op jit(solution)/shard_map/ppermute | solution.py:714
  29.1 12.7 %all-to-all-start = ((f32[128,1,256]{2,1,0:T(1,128)}), f32[128,1,256]{2,1,0:T(1,128)S(1)}, u32[]{:S(2)}, u32[]{:S(2)}) async-start(f32[128,1,256]{2,1,0:T(1,128)} %get-tuple-element.34.refs_1_), calls=%async_computation | async-start | bytes 262144 | tf_op jit(solution)/shard_map/all_to_all | solution.py:712
  41.8 0.0 copy-start
  41.8 14.0 %interact_own.1 = (bf16[1296,2048]{1,0:T(8,128)(2,1)}, f32[8,2048]{1,0:T(8,128)S(1)}) custom-call(bf16[1296,1296]{1,0:T(8,128)(2,1)} %it_hbm.3, bf16[1296,2048]{1,0:T(8,128)(2,1)} %s_hbm.3, f32[128,1,256]{2,1,0:T(1,128)} %get-tuple-element.34.refs_1_), custom_call_target="tpu_custom_call" | custom-call | flops 6879707136 | bytes 10616832 | tf_op jit(solution)/shard_map/interact_own/pallas_call | solution.py:213
  55.8 0.0 copy-start.1
  55.8 0.0 all-to-all-done.got_ref
  55.8 5.3 %stress.1 = (f32[128,1,128]{2,1,0:T(1,128)}, f32[8,2048]{1,0:T(8,128)S(1)}) custom-call(f32[7,72,128]{2,1,0:T(8,128)S(1)} %copy-done, f32[128,1,256]{2,1,0:T(1,128)S(1)} %all-to-all-done.got_ref, f32[8,2048]{1,0:T(8,128)S(1)} %get-tuple-element.35.p_ref, bf16[1296,2048]{1,0:T(8,128)(2,1)} %s_hbm.3, f32[8,2048]{1,0:T(8,128)S(1)} %get-tuple-element.36.wait_ref.mean_ref), custom_call_target="tpu_custom_call" | custom-call | flops 26542080 | bytes 5308416 | tf_op jit(solution)/shard_map/stress/pallas_call | solution.py:390
  61.1 9.8 %all-to-all-start.1 = ((f32[128,1,128]{2,1,0:T(1,128)}), f32[128,1,128]{2,1,0:T(1,128)S(1)}, u32[]{:S(2)}, u32[]{:S(2)}) async-start(f32[128,1,128]{2,1,0:T(1,128)} %get-tuple-element.42), calls=%async_computation.1 | async-start | bytes 131072 | tf_op jit(solution)/shard_map/all_to_all | solution.py:717
  71.0 24.3 %move.1 = (bf16[1296,2048]{1,0:T(8,128)(2,1)}, f32[8,128]{1,0:T(8,128)S(1)}) custom-call(f32[7,72,128]{2,1,0:T(8,128)S(1)} %copy-done, f32[8,2048]{1,0:T(8,128)S(1)} %get-tuple-element.37.winds_ref, s32[4,2048]{1,0:T(4,128)S(1)} %copy-done.1, f32[128,1,256]{2,1,0:T(1,128)S(1)} %all-to-all-done.got_ref, f32[8,2048]{1,0:T(8,128)S(1)} %get-tuple-element.36.wait_ref.mean_ref, ...), custom_call_target="tpu_custom_call" | custom-call | flops 15755378688 | bytes 21233664 | tf_op jit(solution)/shard_map/move/pallas_call | solution.py:613
  95.3 2.4 %cells.1 = (f32[2,64,128]{2,1,0:T(8,128)}, f32[64,128]{1,0:T(8,128)}) custom-call(f32[128,1,128]{2,1,0:T(1,128)S(1)} %all-to-all-done.1.got_ref, s32[128,32]{1,0:T(8,128)S(1)} %bitcast.5, s32[32,128]{1,0:T(8,128)S(1)} %get-tuple-element.30.refs_3_.pusht_ref, f32[2,64,128]{2,1,0:T(8,128)S(1)} %get-tuple-element.43.air_ref, ...), custom_call_target="tpu_custom_call" | custom-call | flops 536870912 | bytes 400000 | tf_op jit(solution)/shard_map/cells/pallas_call | solution.py:669
  (10 shorter events, 0.0 us)
Async XLA Ops:
  0.6 12.1 %copy-start.2 = (f32[2,64,128]{2,1,0:T(8,128)S(1)}, f32[2,64,128]{2,1,0:T(8,128)}, u32[]{:S(2)}) copy-start(f32[2,64,128]{2,1,0:T(8,128)} %param.15) | copy-start | bytes 196612
  0.6 12.1 %copy-start.3 = (f32[64,128]{1,0:T(8,128)S(1)}, f32[64,128]{1,0:T(8,128)}, u32[]{:S(2)}) copy-start(f32[64,128]{1,0:T(8,128)} %param.16) | copy-start | bytes 98308
  1.4 11.3 %collective-permute-start = (f32[3,8,128]{2,1,0:T(8,128)S(1)}, f32[3,8,128]{2,1,0:T(8,128)S(1)}, u32[]{:S(2)}, u32[]{:S(2)}) collective-permute-start(f32[3,8,128]{2,1,0:T(8,128)S(1)} %get-tuple-element.47), channel_id=1, source_target_pairs={{0,1},{1,2},{2,3},{3,4},{4,5},{5,6},{6,7},{8,9},{9,10},{10,11},{11... | collective-permute-start | bytes 36872 | tf_op jit(solution)/shard_map/ppermute | solution.py:701
  6.4 6.3 %collective-permute-start.1 = (f32[3,8,128]{2,1,0:T(8,128)S(1)}, f32[3,8,128]{2,1,0:T(8,128)S(1)}, u32[]{:S(2)}, u32[]{:S(2)}) collective-permute-start(f32[3,8,128]{2,1,0:T(8,128)S(1)} %get-tuple-element.48), channel_id=1, source_target_pairs={{1,0},{2,1},{3,2},{4,3},{5,4},{6,5},{7,6},{9,8},{10,9},{11,10},{12... | collective-permute-start | bytes 36872 | tf_op jit(solution)/shard_map/ppermute | solution.py:702
  12.8 5.6 %collective-permute-start.3 = (f32[3,80,128]{2,1,0:T(8,128)S(1)}, f32[3,80,128]{2,1,0:T(8,128)S(1)}, u32[]{:S(2)}, u32[]{:S(2)}) collective-permute-start(f32[3,80,128]{2,1,0:T(8,128)S(1)} %pad_maximum_fusion.refs_0_), channel_id=1, source_target_pairs={{8,0},{16,8},{24,16},{32,24},{40,32},{48,40},{56,48},{64,56},{72,6... | collective-permute-start | bytes 368648 | tf_op jit(solution)/shard_map/ppermute | solution.py:707
  14.1 5.8 %collective-permute-start.2 = (f32[3,80,128]{2,1,0:T(8,128)S(1)}, f32[3,80,128]{2,1,0:T(8,128)S(1)}, u32[]{:S(2)}, u32[]{:S(2)}) collective-permute-start(f32[3,80,128]{2,1,0:T(8,128)S(1)} %pad_maximum_fusion.refs_0_), channel_id=1, source_target_pairs={{0,8},{8,16},{16,24},{24,32},{32,40},{40,48},{48,56},{56,64},{64,7... | collective-permute-start | bytes 368648 | tf_op jit(solution)/shard_map/ppermute | solution.py:706
  22.1 48.9 %collective-permute-start.4 = (bf16[1312,512]{1,0:T(8,128)(2,1)}, bf16[1312,512]{1,0:T(8,128)(2,1)S(1)}, u32[]{:S(2)}, u32[]{:S(2)}) collective-permute-start(bf16[1312,512]{1,0:T(8,128)(2,1)} %get-tuple-element.38), channel_id=1, source_target_pairs={{0,1},{1,2},{2,3},{3,4},{4,5},{5,6},{6,7},{7,8},{8,9},{9,10},{10,1... | collective-permute-start | bytes 4030472 | tf_op jit(solution)/shard_map/ppermute | solution.py:713
  27.1 43.8 %collective-permute-start.5 = (bf16[1312,512]{1,0:T(8,128)(2,1)S(1)}, bf16[1312,512]{1,0:T(8,128)(2,1)}, u32[]{:S(2)}, u32[]{:S(2)}) collective-permute-start(bf16[1312,512]{1,0:T(8,128)(2,1)S(1)} %get-tuple-element.39), channel_id=1, source_target_pairs={{1,0},{2,1},{3,2},{4,3},{5,4},{6,5},{7,6},{8,7},{9,8},{10,9},{11,1... | collective-permute-start | bytes 4030472 | tf_op jit(solution)/shard_map/ppermute | solution.py:714
  29.1 26.7 %all-to-all-start = ((f32[128,1,256]{2,1,0:T(1,128)}), f32[128,1,256]{2,1,0:T(1,128)S(1)}, u32[]{:S(2)}, u32[]{:S(2)}) async-start(f32[128,1,256]{2,1,0:T(1,128)} %get-tuple-element.34.refs_1_), calls=%async_computation | async-start | bytes 262144 | tf_op jit(solution)/shard_map/all_to_all | solution.py:712
  41.8 14.0 %copy-start = (f32[7,72,128]{2,1,0:T(8,128)S(1)}, f32[7,72,128]{2,1,0:T(8,128)}, u32[]{:S(2)}) copy-start(f32[7,72,128]{2,1,0:T(8,128)} %constant.2.clone.tab_ref) | copy-start | bytes 774148
  55.8 15.2 %copy-start.1 = (s32[4,2048]{1,0:T(4,128)S(1)}, s32[4,2048]{1,0:T(4,128)}, u32[]{:S(2)}) copy-start(s32[4,2048]{1,0:T(4,128)} %link_ref.1) | copy-start | bytes 98308
  61.1 34.1 %all-to-all-start.1 = ((f32[128,1,128]{2,1,0:T(1,128)}), f32[128,1,128]{2,1,0:T(1,128)S(1)}, u32[]{:S(2)}, u32[]{:S(2)}) async-start(f32[128,1,128]{2,1,0:T(1,128)} %get-tuple-element.42), calls=%async_computation.1 | async-start | bytes 131072 | tf_op jit(solution)/shard_map/all_to_all | solution.py:717
